TPU v7x, 256 devices: a whole 4x4x8 slice. The times are simulated.
256 devices in a mesh: seq: 64 (over y, z, core), head: 4 (over x).
Axes of the slice: x: 4, y: 4, z: 8, core: 2. Of those that a mesh axis runs over, the one named last changes fastest.
Arguments:
- queries: float32 [8192, 4096], P('seq', 'head'), may hold values from -6 to 6
- key_rows: float32 [8192, 4096], P('seq', 'head'), may hold values from -6 to 6
- value_rows: float32 [8192, 4096], P('seq', 'head'), may hold values from -6 to 6
- target: float32 [8192, 4096], P('seq', 'head'), may hold values from -6 to 6
- norm_gain: float32 [4096], P('head'), may hold values from 0.1 to 1.9
- valid_mask: int32 [8192], P('seq'), may hold values from 0 to 1, as said below
Outputs:
- grad_queries: float32 [8192, 4096], P('seq', 'head')
- grad_keys: float32 [8192, 4096], P('seq', 'head')
- grad_values: float32 [8192, 4096], P('seq', 'head')
- loss_value: float32 [], replicated
Inputs may be any that keep to these rules, and one draw needn't show every extreme that they name: `valid_mask`: the last token of the sequence is valid.
All inputs are finite; a program needn't handle non-finite values.
Results may differ from a plain program's by a relative error of at most 0.0003.
Values sent between devices are 32-bit elements; how exact they have to be, the bound alone decides.
A program may use at most 64 MiB of HBM per device.

v0:
```python
import functools

import jax
import jax.numpy as jnp
from jax import lax
from jax.sharding import Mesh
from jax.sharding import PartitionSpec as P

HEAD_DIM = 128
WIDTH = 4096
SEQ = ("seq_0", "seq_1", "seq_2")
SEQ_HEAD = ("seq_0", "seq_1", "seq_2", "head")


epsilon = 1e-06


def filled_with(x, identity):
    return jnp.zeros_like(x) + jnp.asarray(identity, x.dtype)


def carried_in(x, axes, combine, identity, reverse):
    before = start = filled_with(x, identity)
    subtotal = x
    for axis in reversed(axes):
        count, here = (lax.axis_size(axis), lax.axis_index(axis))
        pieces = lax.all_gather(subtotal, axis)
        inside, subtotal = (start, start)
        for k in reversed(range(count)) if reverse else range(count):
            passed = k > here if reverse else k < here
            subtotal = combine(subtotal, pieces[k])
            inside = jnp.where(passed, subtotal, inside)
        before = combine(inside, before)
    return before


def sent_to_all(x, axis):
    count = lax.axis_size(axis)
    return lax.all_to_all(jnp.broadcast_to(x[None], (count, *x.shape)), axis, 0, 0, tiled=True)


def taken_together(x, axis):
    everything = sent_to_all(x, axis)
    return jnp.sum(everything, axis=0)


def in_one(arrays, axis):
    flat, at, done = (jnp.concatenate([a.reshape(-1) for a in arrays]), 0, [])
    subtotal = taken_together(flat, axis)
    for a in arrays:
        done.append(subtotal[at : at + a.size].reshape(a.shape))
        at += a.size
    return tuple(done)


def by_axis(x, axes):
    return functools.reduce(lax.psum, axes, x)


def combine_sum(earlier, later):
    return earlier + later


def shards(queries, key_rows, value_rows, target, norm_gain, valid_mask):
    highest = lax.Precision.HIGHEST
    length, columns = queries.shape
    heads_here = columns // HEAD_DIM
    query_heads = queries.reshape(length, heads_here, HEAD_DIM)
    key_heads = key_rows.reshape(length, heads_here, HEAD_DIM)
    value_heads = value_rows.reshape(length, heads_here, HEAD_DIM)
    causal = jnp.tril(jnp.ones((length, length), jnp.float32))
    mask_float = valid_mask.astype(jnp.float32)
    weighted = mask_float[:, None] * target
    local_count = jnp.sum(mask_float)
    scores = jnp.einsum("the,she->hts", query_heads, key_heads, precision=highest) * causal
    local_out = jnp.einsum("hts,shf->thf", scores, value_heads, precision=highest)
    kv_local = jnp.einsum("the,thf->hef", key_heads, value_heads, precision=highest)
    empty_state = jnp.zeros((heads_here, HEAD_DIM, HEAD_DIM), jnp.float32)
    prior_state = carried_in(kv_local, SEQ, combine_sum, empty_state, False)
    attended = local_out + jnp.einsum("the,hef->thf", query_heads, prior_state, precision=highest)
    attended = attended.reshape(length, columns)
    squares = jnp.sum(attended * attended, axis=1)
    dots_local = jnp.sum(norm_gain * weighted * attended, axis=1)
    total_squares, gain_dots = in_one((squares, dots_local), "head")
    inverse_rms = lax.rsqrt(total_squares / WIDTH + epsilon)
    normed = attended * inverse_rms[:, None] * norm_gain
    loss_local = jnp.sum(weighted * normed)
    grad_core = inverse_rms[:, None] * (
        norm_gain * weighted - attended * (inverse_rms * inverse_rms * gain_dots / WIDTH)[:, None]
    )
    whole_tokens = length * lax.axis_size(SEQ)
    grad_heads = grad_core.reshape(length, heads_here, HEAD_DIM)
    grad_local = jnp.einsum("the,thf->hef", query_heads, grad_heads, precision=highest)
    later_state = carried_in(grad_local, SEQ, combine_sum, empty_state, True)
    grad_scores = jnp.einsum("thf,shf->hts", grad_heads, value_heads, precision=highest) * causal
    grad_query = jnp.einsum("hts,she->the", grad_scores, key_heads, precision=highest)
    grad_query = grad_query + jnp.einsum("thf,hef->the", grad_heads, prior_state, precision=highest)
    grad_key = jnp.einsum("hts,the->she", grad_scores, query_heads, precision=highest)
    grad_key = grad_key + jnp.einsum("shf,hef->she", value_heads, later_state, precision=highest)
    grad_value = jnp.einsum("hts,thf->shf", scores, grad_heads, precision=highest)
    grad_value = grad_value + jnp.einsum("she,hef->shf", key_heads, later_state, precision=highest)
    grad_query = grad_query.reshape(length, columns)
    grad_key = grad_key.reshape(length, columns)
    grad_value = grad_value.reshape(length, columns)
    loss_sum, token_total = (
        by_axis(loss_local, SEQ_HEAD),
        by_axis(local_count / lax.axis_size("head"), SEQ_HEAD),
    )
    loss_value = loss_sum / token_total
    scale_factor = whole_tokens / token_total
    grad_query = scale_factor * grad_query
    grad_key = scale_factor * grad_key
    grad_value = scale_factor * grad_value
    return (grad_query, grad_key, grad_value, loss_value)


def solution(mesh):
    finer = Mesh(
        mesh.devices.reshape(4, 8, 2, mesh.shape["head"]), ("seq_0", "seq_1", "seq_2", "head")
    )
    placed = (P(SEQ, "head"), P(SEQ, "head"), P(SEQ, "head"), P(SEQ, "head"), P("head"), P(SEQ))
    return jax.shard_map(
        shards,
        mesh=finer,
        in_specs=placed,
        out_specs=(P(SEQ, "head"), P(SEQ, "head"), P(SEQ, "head"), P()),
        check_vma=False,
    )
```

profile of v0, /device:TPU:1, one launch (start us, length us, event | category | flops | bytes accessed | tf_op | source)
XLA Modules:
  0.0 284.9 jit_solution(10389869019724577367)
XLA Ops:
  7.2 0.0 copy-start
  7.2 0.0 all-gather.15.cloned.1.call-start
  7.2 1.2 copy.120
  8.4 0.2 copy.88
  8.6 0.0 copy-start.4
  8.7 2.7 fusion.9
  11.3 0.0 all-gather.15.cloned.1.call-update
  11.4 0.0 all-gather.19.cloned.1.call-start
  11.4 19.0 %all-gather.15.cloned.1.call-done = f32[16,128,128]{2,1,0:T(8,128)} async-done(((f32[8,128,128]{2,1,0:T(8,128)}), f32[16,128,128]{2,1,0:T(8,128)}) %all-gather.15.cloned.1.call-update) | async-done | bytes 1048592 | tf_op jit(solution)/shard_map/all_gather | solution.py:27
  30.4 0.0 copy-done.4
  30.4 2.0 slice_add_fusion.17
  32.4 0.0 all-gather.19.cloned.1.call-update
  32.5 0.0 all-gather.11.cloned.1.call-start
  32.5 55.4 %all-gather.19.cloned.1.call-done = f32[64,128,128]{2,1,0:T(8,128)} async-done(((f32[8,128,128]{2,1,0:T(8,128)}), f32[64,128,128]{2,1,0:T(8,128)}) %all-gather.19.cloned.1.call-update) | async-done | bytes 4194320 | tf_op jit(solution)/shard_map/all_gather | solution.py:27
  87.9 3.2 %fusion.26 = (f32[1,8,128,128]{3,2,1,0:T(8,128)}, f32[8,128,128]{2,1,0:T(8,128)S(1)}) fusion(f32[64,128,128]{2,1,0:T(8,128)} %all-gather.19.cloned.1.call-done), kind=kLoop, calls=%fused_computation.51 | loop fusion | flops 917504 | bytes 5242880 | tf_op jit(solution)/shard_map/add | solution.py:61
  91.2 0.0 all-gather.11.cloned.1.call-update
  91.2 0.0 all-gather.17.cloned.1.call-start
  91.3 0.0 copy-done.8
  91.3 0.0 copy-done
  91.3 0.0 copy-done.2
  91.3 1.2 convolution_multiply_fusion.1
  92.5 0.0 copy-done.1
  92.5 1.8 convolution_bitcast_fusion.6
  94.3 29.0 %all-gather.11.cloned.1.call-done = f32[4,8,128,128]{3,2,1,0:T(8,128)} async-done(((f32[1,8,128,128]{3,2,1,0:T(8,128)}), f32[4,8,128,128]{3,2,1,0:T(8,128)}) %all-gather.11.cloned.1.call-update) | async-done | bytes 2097168 | tf_op jit(solution)/shard_map/all_gather | solution.py:27
  123.3 0.0 copy-done.5
  123.3 3.6 %fusion.25 = f32[8,128,128]{2,1,0:T(8,128)S(1)} fusion(f32[4,8,128,128]{3,2,1,0:T(8,128)} %all-gather.11.cloned.1.call-done, f32[1,8,128,128]{3,2,1,0:T(8,128)S(1)} %copy-done.5, f32[8,128,128]{2,1,0:T(8,128)S(1)} %get-tuple-element.31, f32[64,128,128]{2,1,0:T(8,128)} %all-gather.19.cloned.1.call-done, f32[16,128,128]{2,1,0:T(8,128)} %all-gather.15.cloned.1.call-done, ...), kind=kLoop, calls=%fused_computation.47 | loop fusion | flops 3276800 | bytes 7864334 | tf_op jit(solution)/shard_map/add | solution.py:61
  126.9 0.0 copy-done.6
  126.9 1.0 multiply_reduce_fusion.2
  128.0 0.2 copy.92
  128.2 0.0 copy-done.7
  128.2 1.3 multiply_reduce_fusion.1
  129.5 7.9 %all_to_all.6 = f32[4,1,256]{2,1,0:T(1,128)S(1)} all-to-all(f32[4,1,256]{2,1,0:T(1,128)S(1)} %broadcast_in_dim.13), channel_id=1, replica_groups=mesh['seq_0'=4,'seq_1'=8,'seq_2'=2,'head'=4] {'head'}, dimensions={0} | all-to-all | bytes 8192 | tf_op jit(solution)/shard_map/all_to_all | solution.py:39
  137.4 1.9 multiply_reduce_fusion
  139.4 0.2 copy.116
  139.6 0.7 convolution_bitcast_fusion.1
  140.2 1.0 copy.102
  141.2 0.0 all-gather.17.cloned.1.call-update
  141.2 0.0 all-gather.21.cloned.1.call-start
  141.3 15.0 %all-gather.17.cloned.1.call-done = f32[16,128,128]{2,1,0:T(8,128)} async-done(((f32[8,128,128]{2,1,0:T(8,128)}), f32[16,128,128]{2,1,0:T(8,128)}) %all-gather.17.cloned.1.call-update) | async-done | bytes 1048592 | tf_op jit(solution)/shard_map/all_gather | solution.py:27
  156.3 2.0 slice_add_fusion.8
  158.3 0.0 all-gather.21.cloned.1.call-update
  158.4 0.0 all-gather.13.cloned.1.call-start
  158.4 55.3 %all-gather.21.cloned.1.call-done = f32[64,128,128]{2,1,0:T(8,128)} async-done(((f32[8,128,128]{2,1,0:T(8,128)}), f32[64,128,128]{2,1,0:T(8,128)}) %all-gather.21.cloned.1.call-update) | async-done | bytes 4194320 | tf_op jit(solution)/shard_map/all_gather | solution.py:27
  213.7 3.4 %fusion.20 = (f32[1,8,128,128]{3,2,1,0:T(8,128)}, f32[8,128,128]{2,1,0:T(8,128)}) fusion(f32[64,128,128]{2,1,0:T(8,128)} %all-gather.21.cloned.1.call-done), kind=kLoop, calls=%fused_computation.34 | loop fusion | flops 917504 | bytes 5242880 | tf_op jit(solution)/shard_map/add | solution.py:61
  217.1 0.0 all-gather.13.cloned.1.call-update
  217.1 0.6 convert_reduce_fusion
  218.4 9.1 %all-reduce.2 = (f32[]{:T(128)}, f32[]{:T(128)}) all-reduce(f32[]{:T(128)S(6)} %div.15, f32[]{:T(128)} %get-tuple-element.32), channel_id=1, replica_groups=mesh['seq_0'=4,'seq_1'=8,'seq_2'=2,'head'=4] {'seq_0'}, use_global_device_ids=true, to_apply=%region_1.2 | all-reduce | flops 2 | bytes 16 | tf_op jit(solution)/shard_map/psum | solution.py:57
  227.5 13.6 %all-reduce = (f32[]{:T(128)}, f32[]{:T(128)}) all-reduce(f32[]{:T(128)} %get-tuple-element.24, f32[]{:T(128)} %get-tuple-element.25), channel_id=1, replica_groups=mesh['seq_0'=4,'seq_1'=8,'seq_2'=2,'head'=4] {'seq_1'}, use_global_device_ids=true, to_apply=%region_2.3 | all-reduce | flops 2 | bytes 16 | tf_op jit(solution)/shard_map/psum | solution.py:57
  241.1 8.2 %all-reduce.3 = (f32[]{:T(128)}, f32[]{:T(128)}) all-reduce(f32[]{:T(128)} %get-tuple-element.20, f32[]{:T(128)} %get-tuple-element.21), channel_id=1, replica_groups=mesh['seq_0'=4,'seq_1'=8,'seq_2'=2,'head'=4] {'seq_2'}, use_global_device_ids=true, to_apply=%region_3.4 | all-reduce | flops 2 | bytes 16 | tf_op jit(solution)/shard_map/psum | solution.py:57
  249.2 9.2 %all-reduce.1 = (f32[]{:T(128)}, f32[]{:T(128)}) all-reduce(f32[]{:T(128)} %get-tuple-element.26, f32[]{:T(128)} %get-tuple-element.27), channel_id=1, replica_groups=mesh['seq_0'=4,'seq_1'=8,'seq_2'=2,'head'=4] {'head'}, use_global_device_ids=true, to_apply=%region_4.5 | all-reduce | flops 2 | bytes 16 | tf_op jit(solution)/shard_map/psum | solution.py:57
  260.5 1.0 convolution_multiply_fusion
  261.5 2.2 convolution_bitcast_fusion.4
  263.7 1.4 fusion.4
  265.2 2.0 copy.108
  267.2 0.6 fusion.44
  267.9 1.0 convolution_bitcast_fusion.2
  268.9 0.0 copy-start.3
  268.9 0.0 all-gather.13.cloned.1.call-done
  268.9 3.8 %fusion.19 = f32[8,128,128]{2,1,0:T(8,128)S(1)} fusion(f32[4,8,128,128]{3,2,1,0:T(8,128)} %all-gather.13.cloned.1.call-done, f32[1,8,128,128]{3,2,1,0:T(8,128)} %get-tuple-element.28, f32[8,128,128]{2,1,0:T(8,128)} %get-tuple-element.29, f32[64,128,128]{2,1,0:T(8,128)} %all-gather.21.cloned.1.call-done, f32[16,128,128]{2,1,0:T(8,128)} %all-gather.17.cloned.1.call-done, ...), kind=kLoop, calls=%fused_computation.30 | loop fusion | flops 3276800 | bytes 7864334 | tf_op jit(solution)/shard_map/add | solution.py:61
  272.7 0.0 copy-done.3
  272.7 1.0 fusion
  273.7 1.2 fusion.2
  275.0 1.0 copy.109
  276.0 1.0 copy.110
  (12 shorter events, 0.1 us)
Async XLA Ops:
  7.2 84.1 %copy-start = (f32[128,1024]{1,0:T(8,128)S(1)}, f32[128,1024]{1,0:T(8,128)}, u32[]{:S(2)}) copy-start(f32[128,1024]{1,0:T(8,128)} %param.6) | copy-start | bytes 1572868
  7.2 23.2 %all-gather.15.cloned.1.call-start = ((), (), s32[]{:S(2)}) async-start(), calls=%async_computation.3 | async-start | bytes 1572864 | tf_op jit(solution)/shard_map/all_gather | solution.py:27
  8.6 21.7 %copy-start.4 = (f32[128,8,128]{0,2,1:T(8,128)}, f32[128,8,128]{0,2,1:T(8,128)S(1)}, u32[]{:S(2)}) copy-start(f32[128,8,128]{0,2,1:T(8,128)S(1)} %copy.88) | copy-start | bytes 1572868
  11.3 79.9 %copy-start.8 = (s32[128]{0:T(128)S(1)}, s32[128]{0:T(128)}, u32[]{:S(2)}) copy-start(s32[128]{0:T(128)} %param.11) | copy-start | bytes 1540
  11.3 80.0 %copy-start.2 = (f32[128,1024]{1,0:T(8,128)S(1)}, f32[128,1024]{1,0:T(8,128)}, u32[]{:S(2)}) copy-start(f32[128,1024]{1,0:T(8,128)} %param.7) | copy-start | bytes 1572868
  11.4 76.6 %all-gather.19.cloned.1.call-start = ((), (), s32[]{:S(2)}) async-start(), calls=%async_computation.5 | async-start | bytes 4718592 | tf_op jit(solution)/shard_map/all_gather | solution.py:27
  32.4 60.1 %copy-start.1 = (f32[128,1024]{1,0:T(8,128)S(1)}, f32[128,1024]{1,0:T(8,128)}, u32[]{:S(2)}) copy-start(f32[128,1024]{1,0:T(8,128)} %param.8) | copy-start | bytes 1572868
  32.5 90.8 %all-gather.11.cloned.1.call-start = ((), (), s32[]{:S(2)}) async-start(), calls=%async_computation.1 | async-start | bytes 2621440 | tf_op jit(solution)/shard_map/all_gather | solution.py:27
  91.1 32.1 %copy-start.5 = (f32[1,8,128,128]{3,2,1,0:T(8,128)S(1)}, f32[1,8,128,128]{3,2,1,0:T(8,128)}, u32[]{:S(2)}) copy-start(f32[1,8,128,128]{3,2,1,0:T(8,128)} %get-tuple-element.30) | copy-start | bytes 1572868
  91.2 65.1 %all-gather.17.cloned.1.call-start = ((), (), s32[]{:S(2)}) async-start(), calls=%async_computation.4 | async-start | bytes 1572864 | tf_op jit(solution)/shard_map/all_gather | solution.py:27
  123.3 3.6 %copy-start.6 = (f32[128,8,128]{0,2,1:T(8,128)S(1)}, f32[128,8,128]{0,2,1:T(8,128)}, u32[]{:S(2)}) copy-start(f32[128,8,128]{0,2,1:T(8,128)} %convolution_bitcast_fusion.6) | copy-start | bytes 1572868
  123.3 4.9 %copy-start.7 = (f32[1024]{0:T(1024)S(1)}, f32[1024]{0:T(1024)}, u32[]{:S(2)}) copy-start(f32[1024]{0:T(1024)} %param.10) | copy-start | bytes 12292
  141.2 72.5 %all-gather.21.cloned.1.call-start = ((), (), s32[]{:S(2)}) async-start(), calls=%async_computation.6 | async-start | bytes 4718592 | tf_op jit(solution)/shard_map/all_gather | solution.py:27
  158.4 110.5 %all-gather.13.cloned.1.call-start = ((), (), s32[]{:S(2)}) async-start(), calls=%async_computation.2 | async-start | bytes 2621440 | tf_op jit(solution)/shard_map/all_gather | solution.py:27
  268.9 3.8 %copy-start.3 = (f32[128,1024]{1,0:T(8,128)S(1)}, f32[128,1024]{1,0:T(8,128)}, u32[]{:S(2)}) copy-start(f32[128,1024]{1,0:T(8,128)} %param.7) | copy-start | bytes 1572868
Sparse Core Ops, SparseCore 0:
  11.5 18.8 all-gather.14
  32.7 55.1 all-gather.18
  91.3 31.9 all-gather.10
  141.4 14.8 all-gather.16
  158.5 55.1 all-gather.20
  217.2 31.9 all-gather.12
where the time goes:
time: 285 us
  waiting for transfers between devices  174 us (61%)
  blocking collectives  47.9 us (17%)
  other arithmetic  22 us (8%)
  between operations  18.2 us (6%)
  matrix products  16 us (6%)
  local copies, waits for them, and re-layouts  6.87 us (2%)
    all_gather x6, waiting for transfers between devices, carried_in(): pieces = lax.all_gather(subtotal, axis)  174 us
    psum x4, blocking collectives, by_axis(): return functools.reduce(lax.psum, axes, x)  40 us
    add x6, other arithmetic, combine_sum(): return earlier + later  18.1 us
    all_to_all x1, blocking collectives, sent_to_all(): lax.all_to_all(jnp.broadcast_to(x[None], (count, *x.shape)), axis, 0, 0,...  7.92 us
  transfers between devices with their start and end apart: 6, of which 5 were waited for; matrix products, arithmetic and copies ran while one was open for 4% of the time, Pallas kernels for 0%

commit v1 on v0

v1 whole, which is shorter than its diff:
```python
import jax
import jax.numpy as jnp
from jax import lax
from jax.experimental import pallas as pl
from jax.experimental.pallas import tpu as pltpu
from jax.sharding import PartitionSpec as P

HEAD_DIM = 128
WIDTH = 4096
TOKENS = 8192
HEADS = 8
OWN = 4
CHUNKS = 2
BOTH = OWN // CHUNKS
YS, ZS, XS = 4, 8, 4
CHIPS = YS * ZS
CHUNK_ROWS = BOTH * HEAD_DIM
ROWS = CHUNK_ROWS // CHIPS
EPSILON = 1e-06

F32 = jnp.float32
BF16 = jnp.bfloat16
MESH = pl.DeviceIdType.MESH
PAIR, OUT, BACK = 0, 2, 4
FORWARD, REVERSE = 0, 6
INPUTS, SUMS, STAT_Z, STAT_Y, RESULTS, COUNT = 12, 17, 18, 19, 20, 23


def ring(delta, count):
    return min(delta, count - delta)


OFFSETS = sorted(
    ((dy, dz) for dy in range(YS) for dz in range(ZS) if dy or dz),
    key=lambda o: -(ring(o[0], YS) + ring(o[1], ZS)),
)


def split(x):
    high = x.astype(BF16)
    return high, (x - high.astype(F32)).astype(BF16)


def dot3(a, b, contract):
    dims = ((contract[:1], contract[1:]), ((), ()))

    def one(x, y):
        return lax.dot_general(x, y, dims, preferred_element_type=F32)

    return one(a[0], b[0]) + (one(a[0], b[1]) + one(a[1], b[0]))


NN, NT, TN = (1, 0), (1, 1), (0, 0)


def kernel(
    q_hbm, k_hbm, v_hbm, t_hbm, gain_ref, mask_ref,
    gq_hbm, gk_hbm, gv_hbm, loss_ref,
    k_all, v_all, q, k, v, t, mask,
    qh, ql, kh, kl, vh, vl, sh, sl, att, g, gq, gk, gv, acc,
    kv, kv_far, other, comb, recv, pre, part,
    qg, qg_one, comb_b, recv_b, pre_b, part_b,
    row_out, row_in, stat_z_out, stat_z, stat_y_out, stat_y,
    load_sems, store_sem, send_sems, recv_sems,
):
    s, x = lax.axis_index("seq"), lax.axis_index("head")
    y, z, c = s // 16, (s // 2) % ZS, s % 2
    me = y * ZS + z
    far = 1 - c

    def at(ty, tz, tc, tx):
        return (ty * 16 + tz * 2 + tc, tx)

    partner = at(y, z, far, x)
    chips = [((y + dy) % YS, (z + dz) % ZS) for dy, dz in OFFSETS]
    across = [at(y, z, tc, (x + d) % XS) for d in (2, 1, 3) for tc in range(2)] + [partner]
    greeted = [at(ty, tz, c, x) for ty, tz in chips] + across
    barrier = pltpu.get_barrier_semaphore()
    for device in greeted:
        pl.semaphore_signal(barrier, inc=1, device_id=device, device_id_type=MESH)

    def heads_of(core):
        return pl.ds(pl.multiple_of(core * OWN * HEAD_DIM, HEAD_DIM), OWN * HEAD_DIM)

    def head(i):
        return pl.ds(pl.multiple_of(i * HEAD_DIM, HEAD_DIM), HEAD_DIM)

    loads = [
        pltpu.make_async_copy(k_hbm, k_all, load_sems.at[0]),
        pltpu.make_async_copy(v_hbm, v_all, load_sems.at[1]),
        pltpu.make_async_copy(q_hbm.at[:, heads_of(c)], q.at[c], load_sems.at[2]),
        pltpu.make_async_copy(t_hbm.at[:, heads_of(c)], t.at[c], load_sems.at[3]),
    ]
    for copy in loads:
        copy.start()

    def send(src, dst, sem, device):
        pltpu.make_async_remote_copy(
            src_ref=src, dst_ref=dst, send_sem=send_sems.at[sem], recv_sem=recv_sems.at[sem],
            device_id=device, device_id_type=MESH,
        ).start()

    def arrived(ref, sem):
        pltpu.make_async_copy(ref, ref, recv_sems.at[sem]).wait()

    def sent(ref, sem):
        pltpu.make_async_copy(ref, ref, send_sems.at[sem]).wait()

    def piece(chunk, i):
        return pl.ds(pl.multiple_of(chunk * CHUNK_ROWS + i * ROWS, ROWS), ROWS)

    all_but_one = pl.ds(0, (CHIPS - 1) * ROWS)

    def rows_of(i):
        return pl.ds(pl.multiple_of(i * HEAD_DIM, HEAD_DIM), HEAD_DIM)

    def spread(comb, recv, base, chunk):
        for ty, tz in chips:
            send(comb.at[piece(chunk, ty * ZS + tz)], recv.at[piece(chunk, me)], base + OUT + chunk, at(ty, tz, c, x))
        recv[piece(chunk, me), :] = comb[piece(chunk, me), :]

    def scan(recv, pre, part, base, chunk, reverse):
        arrived(recv.at[all_but_one], base + OUT + chunk)
        total = jnp.zeros((ROWS, HEAD_DIM), F32)
        for i in reversed(range(CHIPS)) if reverse else range(CHIPS):
            pre[piece(chunk, i), :] = total
            total = total + recv[piece(chunk, i), :]
        for ty, tz in chips:
            send(pre.at[piece(chunk, ty * ZS + tz)], part.at[piece(chunk, me)], base + BACK + chunk, at(ty, tz, c, x))
        part[piece(chunk, me), :] = pre[piece(chunk, me), :]

    def scanned(part, base, chunk):
        arrived(part.at[all_but_one], base + BACK + chunk)

    loads[0].wait()
    loads[1].wait()

    def outer_far(i, carry):
        columns = head(far * OWN + i)
        kv_far[i] = dot3(split(k_all[:, columns]), split(v_all[:, columns]), TN)
        return carry

    def outer_own(i, carry):
        columns = head(c * OWN + i)
        key, value = split(k_all[:, columns]), split(v_all[:, columns])
        kh[c, i], kl[c, i] = key
        vh[c, i], vl[c, i] = value
        kv[i] = dot3(key, value, TN)
        return carry

    lax.fori_loop(0, OWN, outer_far, 0, unroll=2)
    lax.fori_loop(0, OWN, outer_own, 0, unroll=2)
    pl.semaphore_wait(barrier, len(greeted))
    for chunk in range(CHUNKS):
        half = pl.ds(chunk * BOTH, BOTH)
        send(kv_far.at[half], other.at[half], FORWARD + PAIR + chunk, partner)
    for chunk in range(CHUNKS):
        arrived(other.at[pl.ds(0, BOTH)], FORWARD + PAIR + chunk)
        for i in range(chunk * BOTH, (chunk + 1) * BOTH):
            comb[rows_of(i), :] = kv[i] + other[i]
        spread(comb, recv, FORWARD, chunk)

    send(q_hbm.at[:, heads_of(far)], q.at[c], INPUTS, partner)
    send(k_hbm.at[:, heads_of(far)], k, INPUTS + 1, partner)
    send(v_hbm.at[:, heads_of(far)], v, INPUTS + 2, partner)
    send(t_hbm.at[:, heads_of(far)], t.at[c], INPUTS + 3, partner)
    mask[c] = jnp.broadcast_to(mask_ref[...].astype(F32), (8, HEAD_DIM))
    send(mask.at[c], mask.at[c], INPUTS + 4, partner)

    token = lax.broadcasted_iota(jnp.int32, (HEAD_DIM, HEAD_DIM), 0)
    column = lax.broadcasted_iota(jnp.int32, (HEAD_DIM, HEAD_DIM), 1)
    causal = token >= column

    def as_columns(row):
        return jnp.transpose(jnp.broadcast_to(row, (HEAD_DIM, HEAD_DIM)))

    def local(b, i, mask_columns):
        query = split(q[b, :, head(i)])
        qh[b, i], ql[b, i] = query
        scores = jnp.where(causal, dot3(query, (kh[b, i], kl[b, i]), NT), 0.0)
        scores = split(scores)
        sh[b, i], sl[b, i] = scores
        att[b, i] = dot3(scores, (vh[b, i], vl[b, i]), NN)
        t[b, :, head(i)] = gain_ref[pl.ds(c * OWN + i, 1), :] * (mask_columns * t[b, :, head(i)])

    loads[2].wait()
    loads[3].wait()
    mask_near = as_columns(mask[c, 0:1])

    def local_near(i, carry):
        local(c, i, mask_near)
        return carry

    lax.fori_loop(0, OWN, local_near, 0)
    arrived(q.at[0], INPUTS)
    arrived(k, INPUTS + 1)
    arrived(v, INPUTS + 2)
    arrived(t.at[0], INPUTS + 3)
    arrived(mask.at[0], INPUTS + 4)
    mask_far = as_columns(mask[far, 0:1])

    def kv_zero(i):
        return jnp.where(c == 0, kv[i], other[i])

    def local_far(i, carry):
        kh[far, i], kl[far, i] = split(k[:, head(i)])
        vh[far, i], vl[far, i] = split(v[:, head(i)])
        local(far, i, mask_far)
        att[1, i] = att[1, i] + dot3((qh[1, i], ql[1, i]), split(kv_zero(i)), NN)
        return carry

    lax.fori_loop(0, OWN, local_far, 0)
    for chunk in range(CHUNKS):
        scan(recv, pre, part, FORWARD, chunk, False)
    acc[...] = jnp.zeros_like(acc)

    def attend(i, carry):
        prior = split(part[rows_of(i), :])
        for b in range(2):
            row = att[b, i] + dot3((qh[b, i], ql[b, i]), prior, NN)
            att[b, i] = row
            acc[b] = acc[b] + row * row
            acc[2 + b] = acc[2 + b] + t[b, :, head(i)] * row
        return carry

    for chunk in range(CHUNKS):
        scanned(part, FORWARD, chunk)
        lax.fori_loop(chunk * BOTH, (chunk + 1) * BOTH, attend, 0, unroll=True)
    row_out[...] = jnp.zeros_like(row_out)
    for n in range(4):
        row_out[pl.ds(n, 1), :] = jnp.sum(jnp.transpose(acc[n]), axis=0, keepdims=True)
    for device in across:
        send(row_out, row_in.at[x * 2 + c], SUMS, device)
    row_in[x * 2 + c] = row_out[...]
    arrived(row_in.at[pl.ds(0, 2 * XS - 1)], SUMS)
    rows = jnp.sum(row_in[...], axis=0)
    inverse = lax.rsqrt(rows[0:2] / WIDTH + EPSILON)
    gain_dots = rows[2:4]
    slope = inverse * inverse * gain_dots / WIDTH
    inverse_columns = [as_columns(inverse[b : b + 1]) for b in range(2)]
    slope_columns = [as_columns(slope[b : b + 1]) for b in range(2)]

    def outer_qg(i, carry):
        outer = []
        for b in range(2):
            grad = inverse_columns[b] * (t[b, :, head(i)] - att[b, i] * slope_columns[b])
            g[b, i] = grad
            outer.append(dot3((qh[b, i], ql[b, i]), split(grad), TN))
        qg_one[i] = outer[1]
        comb_b[rows_of(i), :] = outer[0] + outer[1]
        return carry

    for chunk in range(CHUNKS):
        lax.fori_loop(chunk * BOTH, (chunk + 1) * BOTH, outer_qg, 0, unroll=True)
        spread(comb_b, recv_b, REVERSE, chunk)
    stat_z_out[...] = jnp.zeros_like(stat_z_out)
    stat_z_out[pl.ds(0, 1), :] = jnp.sum(inverse * gain_dots, axis=0, keepdims=True)
    stat_z_out[pl.ds(1, 1), :] = mask[0, 0:1] + mask[1, 0:1]
    for d in range(1, ZS):
        send(stat_z_out, stat_z.at[z], STAT_Z, at(y, (z + d) % ZS, c, x))
    stat_z[z] = stat_z_out[...]

    def local_grads(i, carry):
        prior = part[rows_of(i), :]
        for b in range(2):
            grad = split(g[b, i])
            query, key, value = (qh[b, i], ql[b, i]), (kh[b, i], kl[b, i]), (vh[b, i], vl[b, i])
            grad_scores = split(jnp.where(causal, dot3(grad, value, NT), 0.0))
            before = split(prior if b == 0 else prior + kv_zero(i))
            gq[b, i] = dot3(grad_scores, key, NN) + dot3(grad, before, NT)
            grad_key = dot3(grad_scores, query, TN)
            grad_value = dot3((sh[b, i], sl[b, i]), grad, TN)
            if b == 0:
                after = split(qg_one[i])
                grad_key = grad_key + dot3(value, after, NT)
                grad_value = grad_value + dot3(key, after, NN)
            gk[b, i] = grad_key
            gv[b, i] = grad_value
        return carry

    lax.fori_loop(0, OWN - 1, local_grads, 0)
    for chunk in range(CHUNKS):
        scan(recv_b, pre_b, part_b, REVERSE, chunk, True)
    arrived(stat_z.at[pl.ds(0, ZS - 1)], STAT_Z)
    stat_y_out[...] = jnp.sum(stat_z[...], axis=0)
    for d in range(1, YS):
        send(stat_y_out, stat_y.at[y], STAT_Y, at((y + d) % YS, z, c, x))
    stat_y[y] = stat_y_out[...]
    lax.fori_loop(OWN - 1, OWN, local_grads, 0)
    arrived(stat_y.at[pl.ds(0, YS - 1)], STAT_Y)
    totals = jnp.sum(stat_y[...], axis=0)
    token_total = jnp.sum(totals[1:2], axis=1, keepdims=True)
    loss_ref[...] = jnp.sum(totals[0:1], axis=1, keepdims=True) / token_total
    scale = TOKENS / token_total

    def store(vmem, hbm, i, sem):
        columns = head(c * OWN + i)
        pltpu.make_async_copy(vmem.at[c, i], hbm.at[:, columns], store_sem).start()
        send(vmem.at[far, i], hbm.at[:, columns], sem, partner)

    def scaled(i, carry):
        for b in range(2):
            gq[b, i] = gq[b, i] * scale
        store(gq, gq_hbm, i, RESULTS)
        return carry

    lax.fori_loop(0, OWN, scaled, 0)

    def last(i, carry):
        later = split(part_b[rows_of(i), :])
        for b in range(2):
            gk[b, i] = (gk[b, i] + dot3((vh[b, i], vl[b, i]), later, NT)) * scale
            gv[b, i] = (gv[b, i] + dot3((kh[b, i], kl[b, i]), later, NN)) * scale
        store(gk, gk_hbm, i, RESULTS + 1)
        store(gv, gv_hbm, i, RESULTS + 2)
        return carry

    for chunk in range(CHUNKS):
        scanned(part_b, REVERSE, chunk)
        lax.fori_loop(chunk * BOTH, (chunk + 1) * BOTH, last, 0, unroll=True)
    for base, flat in ((FORWARD, comb), (REVERSE, comb_b)):
        for chunk in range(CHUNKS):
            sent(flat.at[all_but_one], base + OUT + chunk)
            sent(flat.at[all_but_one], base + BACK + chunk)
            if base == FORWARD:
                sent(kv_far.at[pl.ds(0, BOTH)], base + PAIR + chunk)
    for n in range(4):
        sent(k, INPUTS + n)
    sent(mask.at[0], INPUTS + 4)
    sent(row_in.at[pl.ds(0, 2 * XS - 1)], SUMS)
    sent(stat_z.at[pl.ds(0, ZS - 1)], STAT_Z)
    sent(stat_y.at[pl.ds(0, YS - 1)], STAT_Y)
    for n, done in enumerate((gq, gk, gv)):
        sent(done.at[0], RESULTS + n)
        pltpu.make_async_copy(done.at[0], done.at[0], store_sem).wait()
        arrived(done.at[0], RESULTS + n)


def shards(queries, key_rows, value_rows, target, norm_gain, valid_mask):
    whole = jax.ShapeDtypeStruct(queries.shape, F32)
    full = pltpu.VMEM((HEAD_DIM, HEADS * HEAD_DIM), F32)
    half = pltpu.VMEM((HEAD_DIM, OWN * HEAD_DIM), F32)
    halves = pltpu.VMEM((2, HEAD_DIM, OWN * HEAD_DIM), F32)
    heads = pltpu.VMEM((2, OWN, HEAD_DIM, HEAD_DIM), F32)
    heads16 = pltpu.VMEM((2, OWN, HEAD_DIM, HEAD_DIM), BF16)
    states = pltpu.VMEM((OWN, HEAD_DIM, HEAD_DIM), F32)
    flat = pltpu.VMEM((OWN * HEAD_DIM, HEAD_DIM), F32)

    def tiles(count):
        return pltpu.VMEM((count, 8, HEAD_DIM), F32)

    tile = pltpu.VMEM((8, HEAD_DIM), F32)
    anywhere = pl.BlockSpec(memory_space=pl.ANY)
    vmem = pl.BlockSpec(memory_space=pltpu.VMEM)
    grad_q, grad_k, grad_v, loss = pl.pallas_call(
        kernel,
        out_shape=(whole, whole, whole, jax.ShapeDtypeStruct((1, 1), F32)),
        in_specs=[anywhere] * 4 + [vmem] * 2,
        out_specs=(anywhere, anywhere, anywhere, vmem),
        scratch_shapes=[full, full, halves, half, half, halves, tiles(2)]
        + [heads16] * 8
        + [heads] * 5
        + [pltpu.VMEM((4, HEAD_DIM, HEAD_DIM), F32)]
        + [states] * 3
        + [flat] * 4
        + [states] * 2
        + [flat] * 4
        + [tile, tiles(2 * XS), tile, tiles(ZS), tile, tiles(YS)]
        + [
            pltpu.SemaphoreType.DMA((4,)),
            pltpu.SemaphoreType.DMA,
            pltpu.SemaphoreType.DMA((COUNT,)),
            pltpu.SemaphoreType.DMA((COUNT,)),
        ],
        compiler_params=pltpu.CompilerParams(collective_id=0, has_side_effects=True),
        name="linear_attention",
    )(
        queries, key_rows, value_rows, target,
        norm_gain.reshape(HEADS, HEAD_DIM), valid_mask.reshape(1, HEAD_DIM),
    )
    return grad_q, grad_k, grad_v, loss.reshape(())


def solution(mesh):
    return jax.shard_map(
        shards,
        mesh=mesh,
        in_specs=(P("seq", "head"),) * 4 + (P("head"), P("seq")),
        out_specs=(P("seq", "head"),) * 3 + (P(),),
        check_vma=False,
    )
```

time: 285 us -> 58.9 us (0.21)
  waiting for transfers between devices: 174 us -> 0 us
  Pallas kernels: 0 us -> 52.3 us
  blocking collectives: 47.9 us -> 0 us
  other arithmetic: 22 us -> 0 us
  matrix products: 16 us -> 0 us
  between operations: 18.2 us -> 2.41 us
  local copies, waits for them, and re-layouts: 6.87 us -> 3.97 us
    all_gather x6 -> x0, waiting for transfers between devices: 174 us -> none  [carried_in(): pieces = lax.all_gather(subtotal, axis)]
    pallas_call x0 -> x1, Pallas kernels: none -> 52.3 us  [shards(): pl.pallas_call(kernel, out_shape=(whole, whole, whole, jax.ShapeDtypeStru...]
    psum x4 -> x0, blocking collectives: 40 us -> none  [by_axis(): return functools.reduce(lax.psum, axes, x)]
    add x6 -> x0, other arithmetic: 18.1 us -> none  [combine_sum(): return earlier + later]
    dot_general x12 -> x0, matrix products: 16 us -> none  [the longest x1 2.66 us: shards(): jnp.einsum('the,thf->hef', key_heads, value_heads, precision=highest)]
    all_to_all x1 -> x0, blocking collectives: 7.92 us -> none  [sent_to_all(): lax.all_to_all(jnp.broadcast_to(x[None], (count, *x.shape)), axis, 0, 0,...]
    reduce_sum x4 -> x0, other arithmetic: 3.82 us -> none  [the longest x1 1.94 us: shards(): loss_local = jnp.sum(weighted * normed)]
  transfers between devices with their start and end apart: 6 -> 0, of which waited for: 5 -> 0; matrix products, arithmetic and copies ran while one was open for 4% -> 0% of each run, Pallas kernels for 0% -> 0%
where the time goes in v1:
time: 58.9 us; the launch traced here: 58.7 us
  Pallas kernels  52.3 us (89%)
  local copies, waits for them, and re-layouts  3.97 us (7%)
  between operations  2.41 us (4%)
    pallas_call x1, Pallas kernels, shards(): pl.pallas_call(kernel, out_shape=(whole, whole, whole, jax.ShapeDtypeStru...  52.3 us
    unnamed x7, local copies, waits for them, and re-layouts  3.97 us

profile of v1, /device:TPU:1, one launch (start us, length us, event | category | flops | bytes accessed | tf_op | source)
XLA Modules:
  0.0 58.7 jit_solution(5072472689029089952)
XLA Ops:
  0.6 52.3 %linear_attention.1 = (f32[128,1024]{1,0:T(8,128)}, f32[128,1024]{1,0:T(8,128)}, f32[128,1024]{1,0:T(8,128)}, f32[1,1]{1,0:T(1,128)}) custom-call(f32[128,1024]{1,0:T(8,128)} %q_hbm.1, f32[128,1024]{1,0:T(8,128)} %k_hbm.1, f32[128,1024]{1,0:T(8,128)} %v_hbm.1, f32[128,1024]{1,0:T(8,128)} %t_hbm.1, f32[8,128]{1,0:T(8,128)} %bitcast.3, s32[1,128]{1,0:T(1,128)} %bitcast.4), custom_call_target="tpu_custom_call" | custom-call | tf_op jit(solution)/shard_map/linear_attention/pallas_call | solution.py:355
  53.0 0.0 copy-start.1
  53.0 1.9 %copy.14 = f32[128,1024]{1,0:T(8,128)} copy(f32[128,1024]{1,0:T(8,128)} %get-tuple-element.16) | data formatting | bytes 1048576
  54.9 0.0 copy-done.1
  54.9 0.0 copy-start
  54.9 0.8 %copy.15 = f32[128,1024]{1,0:T(8,128)} copy(f32[128,1024]{1,0:T(8,128)S(1)} %copy-done.1) | data formatting | bytes 1048576
  55.7 0.4 copy-done
  56.1 0.8 %copy.16 = f32[128,1024]{1,0:T(8,128)} copy(f32[128,1024]{1,0:T(8,128)S(1)} %copy-done) | data formatting | bytes 1048576
Async XLA Ops:
  53.0 2.0 %copy-start.1 = (f32[128,1024]{1,0:T(8,128)S(1)}, f32[128,1024]{1,0:T(8,128)}, u32[]{:S(2)}) copy-start(f32[128,1024]{1,0:T(8,128)} %get-tuple-element.17) | copy-start | bytes 1572868
  54.9 1.2 %copy-start = (f32[128,1024]{1,0:T(8,128)S(1)}, f32[128,1024]{1,0:T(8,128)}, u32[]{:S(2)}) copy-start(f32[128,1024]{1,0:T(8,128)} %get-tuple-element.18) | copy-start | bytes 1572868

commit v2 on v1

--- a/solution.py
+++ b/solution.py
@@ -17,13 +17,14 @@
 CHUNK_ROWS = BOTH * HEAD_DIM
 ROWS = CHUNK_ROWS // CHIPS
 EPSILON = 1e-06
+VMEM_LIMIT = 24 * 2**20
 
 F32 = jnp.float32
 BF16 = jnp.bfloat16
 MESH = pl.DeviceIdType.MESH
-PAIR, OUT, BACK = 0, 2, 4
-FORWARD, REVERSE = 0, 6
-INPUTS, SUMS, STAT_Z, STAT_Y, RESULTS, COUNT = 12, 17, 18, 19, 20, 23
+PAIR, OUT, BACK = 0, CHUNKS, 2 * CHUNKS
+FORWARD, REVERSE, INPUTS = 0, 3 * CHUNKS, 6 * CHUNKS
+SUMS, STAT_Z, STAT_Y, RESULTS, COUNT = INPUTS + 5, INPUTS + 6, INPUTS + 7, INPUTS + 8, INPUTS + 11
 
 
 def ring(delta, count):
@@ -54,14 +55,14 @@
 
 
 def kernel(
-    q_hbm, k_hbm, v_hbm, t_hbm, gain_ref, mask_ref,
-    gq_hbm, gk_hbm, gv_hbm, loss_ref,
-    k_all, v_all, q, k, v, t, mask,
+    q_hbm, k_hbm, v_hbm, t_hbm, gain_hbm, mask_hbm,
+    gq_out, gk_out, gv_out, loss_hbm,
+    k_all, v_all, q, k, v, t, gain, mask_row, mask, loss,
     qh, ql, kh, kl, vh, vl, sh, sl, att, g, gq, gk, gv, acc,
     kv, kv_far, other, comb, recv, pre, part,
     qg, qg_one, comb_b, recv_b, pre_b, part_b,
     row_out, row_in, stat_z_out, stat_z, stat_y_out, stat_y,
-    load_sems, store_sem, send_sems, recv_sems,
+    load_sems, send_sems, recv_sems,
 ):
     s, x = lax.axis_index("seq"), lax.axis_index("head")
     y, z, c = s // 16, (s // 2) % ZS, s % 2
@@ -75,10 +76,6 @@
     chips = [((y + dy) % YS, (z + dz) % ZS) for dy, dz in OFFSETS]
     across = [at(y, z, tc, (x + d) % XS) for d in (2, 1, 3) for tc in range(2)] + [partner]
     greeted = [at(ty, tz, c, x) for ty, tz in chips] + across
-    barrier = pltpu.get_barrier_semaphore()
-    for device in greeted:
-        pl.semaphore_signal(barrier, inc=1, device_id=device, device_id_type=MESH)
-
     def heads_of(core):
         return pl.ds(pl.multiple_of(core * OWN * HEAD_DIM, HEAD_DIM), OWN * HEAD_DIM)
 
@@ -90,9 +87,15 @@
         pltpu.make_async_copy(v_hbm, v_all, load_sems.at[1]),
         pltpu.make_async_copy(q_hbm.at[:, heads_of(c)], q.at[c], load_sems.at[2]),
         pltpu.make_async_copy(t_hbm.at[:, heads_of(c)], t.at[c], load_sems.at[3]),
+        pltpu.make_async_copy(gain_hbm, gain, load_sems.at[4]),
+        pltpu.make_async_copy(mask_hbm, mask_row, load_sems.at[5]),
     ]
     for copy in loads:
         copy.start()
+
+    barrier = pltpu.get_barrier_semaphore()
+    for device in greeted:
+        pl.semaphore_signal(barrier, inc=1, device_id=device, device_id_type=MESH)
 
     def send(src, dst, sem, device):
         pltpu.make_async_remote_copy(
@@ -164,7 +167,9 @@
     send(k_hbm.at[:, heads_of(far)], k, INPUTS + 1, partner)
     send(v_hbm.at[:, heads_of(far)], v, INPUTS + 2, partner)
     send(t_hbm.at[:, heads_of(far)], t.at[c], INPUTS + 3, partner)
-    mask[c] = jnp.broadcast_to(mask_ref[...].astype(F32), (8, HEAD_DIM))
+    loads[4].wait()
+    loads[5].wait()
+    mask[c] = jnp.broadcast_to(mask_row[...].astype(F32), (8, HEAD_DIM))
     send(mask.at[c], mask.at[c], INPUTS + 4, partner)
 
     token = lax.broadcasted_iota(jnp.int32, (HEAD_DIM, HEAD_DIM), 0)
@@ -181,7 +186,7 @@
         scores = split(scores)
         sh[b, i], sl[b, i] = scores
         att[b, i] = dot3(scores, (vh[b, i], vl[b, i]), NN)
-        t[b, :, head(i)] = gain_ref[pl.ds(c * OWN + i, 1), :] * (mask_columns * t[b, :, head(i)])
+        t[b, :, head(i)] = gain[pl.ds(c * OWN + i, 1), :] * (mask_columns * t[b, :, head(i)])
 
     loads[2].wait()
     loads[3].wait()
@@ -237,6 +242,12 @@
     inverse = lax.rsqrt(rows[0:2] / WIDTH + EPSILON)
     gain_dots = rows[2:4]
     slope = inverse * inverse * gain_dots / WIDTH
+    stat_z_out[...] = jnp.zeros_like(stat_z_out)
+    stat_z_out[pl.ds(0, 1), :] = jnp.sum(inverse * gain_dots, axis=0, keepdims=True)
+    stat_z_out[pl.ds(1, 1), :] = mask[0, 0:1] + mask[1, 0:1]
+    for d in range(1, ZS):
+        send(stat_z_out, stat_z.at[z], STAT_Z, at(y, (z + d) % ZS, c, x))
+    stat_z[z] = stat_z_out[...]
     inverse_columns = [as_columns(inverse[b : b + 1]) for b in range(2)]
     slope_columns = [as_columns(slope[b : b + 1]) for b in range(2)]
 
@@ -253,13 +264,6 @@
     for chunk in range(CHUNKS):
         lax.fori_loop(chunk * BOTH, (chunk + 1) * BOTH, outer_qg, 0, unroll=True)
         spread(comb_b, recv_b, REVERSE, chunk)
-    stat_z_out[...] = jnp.zeros_like(stat_z_out)
-    stat_z_out[pl.ds(0, 1), :] = jnp.sum(inverse * gain_dots, axis=0, keepdims=True)
-    stat_z_out[pl.ds(1, 1), :] = mask[0, 0:1] + mask[1, 0:1]
-    for d in range(1, ZS):
-        send(stat_z_out, stat_z.at[z], STAT_Z, at(y, (z + d) % ZS, c, x))
-    stat_z[z] = stat_z_out[...]
-
     def local_grads(i, carry):
         prior = part[rows_of(i), :]
         for b in range(2):
@@ -278,41 +282,38 @@
             gv[b, i] = grad_value
         return carry
 
-    lax.fori_loop(0, OWN - 1, local_grads, 0)
-    for chunk in range(CHUNKS):
-        scan(recv_b, pre_b, part_b, REVERSE, chunk, True)
+    lax.fori_loop(0, OWN, local_grads, 0)
     arrived(stat_z.at[pl.ds(0, ZS - 1)], STAT_Z)
     stat_y_out[...] = jnp.sum(stat_z[...], axis=0)
     for d in range(1, YS):
         send(stat_y_out, stat_y.at[y], STAT_Y, at((y + d) % YS, z, c, x))
     stat_y[y] = stat_y_out[...]
-    lax.fori_loop(OWN - 1, OWN, local_grads, 0)
+    for chunk in range(CHUNKS):
+        scan(recv_b, pre_b, part_b, REVERSE, chunk, True)
     arrived(stat_y.at[pl.ds(0, YS - 1)], STAT_Y)
     totals = jnp.sum(stat_y[...], axis=0)
     token_total = jnp.sum(totals[1:2], axis=1, keepdims=True)
-    loss_ref[...] = jnp.sum(totals[0:1], axis=1, keepdims=True) / token_total
+    loss[...] = jnp.sum(totals[0:1], axis=1, keepdims=True) / token_total
+    out_loss = pltpu.make_async_copy(loss, loss_hbm, load_sems.at[6])
+    out_loss.start()
     scale = TOKENS / token_total
 
-    def store(vmem, hbm, i, sem):
+    def store(block, out, i, sem, finished):
         columns = head(c * OWN + i)
-        pltpu.make_async_copy(vmem.at[c, i], hbm.at[:, columns], store_sem).start()
-        send(vmem.at[far, i], hbm.at[:, columns], sem, partner)
+        block[far, i] = finished(far)
+        send(block.at[far, i], out.at[:, columns], sem, partner)
+        out[:, columns] = finished(c)
 
     def scaled(i, carry):
-        for b in range(2):
-            gq[b, i] = gq[b, i] * scale
-        store(gq, gq_hbm, i, RESULTS)
+        store(gq, gq_out, i, RESULTS, lambda b: gq[b, i] * scale)
         return carry
 
     lax.fori_loop(0, OWN, scaled, 0)
 
     def last(i, carry):
         later = split(part_b[rows_of(i), :])
-        for b in range(2):
-            gk[b, i] = (gk[b, i] + dot3((vh[b, i], vl[b, i]), later, NT)) * scale
-            gv[b, i] = (gv[b, i] + dot3((kh[b, i], kl[b, i]), later, NN)) * scale
-        store(gk, gk_hbm, i, RESULTS + 1)
-        store(gv, gv_hbm, i, RESULTS + 2)
+        store(gk, gk_out, i, RESULTS + 1, lambda b: (gk[b, i] + dot3((vh[b, i], vl[b, i]), later, NT)) * scale)
+        store(gv, gv_out, i, RESULTS + 2, lambda b: (gv[b, i] + dot3((kh[b, i], kl[b, i]), later, NN)) * scale)
         return carry
 
     for chunk in range(CHUNKS):
@@ -332,8 +333,17 @@
     sent(stat_y.at[pl.ds(0, YS - 1)], STAT_Y)
     for n, done in enumerate((gq, gk, gv)):
         sent(done.at[0], RESULTS + n)
-        pltpu.make_async_copy(done.at[0], done.at[0], store_sem).wait()
         arrived(done.at[0], RESULTS + n)
+    out_loss.wait()
+
+
+def hand_out(*refs):
+    given, outs, sems = refs[:3], refs[3:6], refs[6]
+    copies = [pltpu.make_async_copy(given[n], outs[n], sems.at[n]) for n in range(3)]
+    for copy in copies:
+        copy.start()
+    for copy in copies:
+        copy.wait()
 
 
 def shards(queries, key_rows, value_rows, target, norm_gain, valid_mask):
@@ -350,14 +360,17 @@
         return pltpu.VMEM((count, 8, HEAD_DIM), F32)
 
     tile = pltpu.VMEM((8, HEAD_DIM), F32)
-    anywhere = pl.BlockSpec(memory_space=pl.ANY)
+    anywhere = pl.BlockSpec(memory_space=pltpu.HBM)
     vmem = pl.BlockSpec(memory_space=pltpu.VMEM)
+    arrays = (queries, key_rows, value_rows, target)
+    arrays += (norm_gain.reshape(HEADS, HEAD_DIM), valid_mask.reshape(1, HEAD_DIM))
     grad_q, grad_k, grad_v, loss = pl.pallas_call(
         kernel,
         out_shape=(whole, whole, whole, jax.ShapeDtypeStruct((1, 1), F32)),
-        in_specs=[anywhere] * 4 + [vmem] * 2,
-        out_specs=(anywhere, anywhere, anywhere, vmem),
-        scratch_shapes=[full, full, halves, half, half, halves, tiles(2)]
+        in_specs=[anywhere] * 6,
+        out_specs=(vmem, vmem, vmem, anywhere),
+        scratch_shapes=[full, full, halves, half, half, halves, tile, pltpu.VMEM((1, HEAD_DIM), jnp.int32), tiles(2)]
+        + [pltpu.VMEM((1, 1), F32)]
         + [heads16] * 8
         + [heads] * 5
         + [pltpu.VMEM((4, HEAD_DIM, HEAD_DIM), F32)]
@@ -367,17 +380,26 @@
         + [flat] * 4
         + [tile, tiles(2 * XS), tile, tiles(ZS), tile, tiles(YS)]
         + [
-            pltpu.SemaphoreType.DMA((4,)),
-            pltpu.SemaphoreType.DMA,
+            pltpu.SemaphoreType.DMA((7,)),
             pltpu.SemaphoreType.DMA((COUNT,)),
             pltpu.SemaphoreType.DMA((COUNT,)),
         ],
-        compiler_params=pltpu.CompilerParams(collective_id=0, has_side_effects=True),
+        compiler_params=pltpu.CompilerParams(
+            collective_id=0, has_side_effects=True, vmem_limit_bytes=VMEM_LIMIT
+        ),
         name="linear_attention",
     )(
-        queries, key_rows, value_rows, target,
-        norm_gain.reshape(HEADS, HEAD_DIM), valid_mask.reshape(1, HEAD_DIM),
+        *[pltpu.with_memory_space_constraint(array, pltpu.HBM) for array in arrays],
     )
+    grad_q, grad_k, grad_v = pl.pallas_call(
+        hand_out,
+        out_shape=(whole,) * 3,
+        in_specs=[vmem] * 3,
+        out_specs=(anywhere,) * 3,
+        scratch_shapes=[pltpu.SemaphoreType.DMA((3,))],
+        compiler_params=pltpu.CompilerParams(vmem_limit_bytes=4 * 2**20),
+        name="hand_out",
+    )(grad_q, grad_k, grad_v)
     return grad_q, grad_k, grad_v, loss.reshape(())
 
 

time: 58.9 us -> 55.3 us (0.939)
  local copies, waits for them, and re-layouts: 3.97 us -> 0 us
    unnamed x7 -> x0, local copies, waits for them, and re-layouts: 3.97 us -> none
    pallas_call x0 -> x1, Pallas kernels: none -> 1.17 us  [shards(): pl.pallas_call(hand_out, out_shape=(whole,) * 3, in_specs=[vmem] * 3, out...]
    pallas_call x1, Pallas kernels: 52.3 us -> 51.6 us  [shards(): pl.pallas_call(kernel, out_shape=(whole, whole, whole, jax.ShapeDtypeStru...]
where the time goes in v2:
time: 55.3 us; the launch traced here: 55.2 us
  Pallas kernels  52.8 us (95%)
  between operations  2.41 us (4%)
    pallas_call x1, Pallas kernels, shards(): pl.pallas_call(kernel, out_shape=(whole, whole, whole, jax.ShapeDtypeStru...  51.6 us
    pallas_call x1, Pallas kernels, shards(): pl.pallas_call(hand_out, out_shape=(whole,) * 3, in_specs=[vmem] * 3, out...  1.17 us

profile of v2, /device:TPU:1, one launch (start us, length us, event | category | flops | bytes accessed | tf_op | source)
XLA Modules:
  0.0 55.2 jit_solution(14501111659128012103)
XLA Ops:
  0.6 51.6 %linear_attention.1 = (f32[128,1024]{1,0:T(8,128)S(1)}, f32[128,1024]{1,0:T(8,128)S(1)}, f32[128,1024]{1,0:T(8,128)S(1)}, f32[1,1]{1,0:T(1,128)}) custom-call(f32[128,1024]{1,0:T(8,128)} %q_hbm.1, f32[128,1024]{1,0:T(8,128)} %k_hbm.1, f32[128,1024]{1,0:T(8,128)} %v_hbm.1, f32[128,1024]{1,0:T(8,128)} %t_hbm.1, f32[8,128]{1,0:T(8,128)} %bitcast.3, ...), custom_call_target="tpu_custom_call" | custom-call | tf_op jit(solution)/shard_map/linear_attention/pallas_call | solution.py:367
  52.3 1.2 %hand_out.1 = (f32[128,1024]{1,0:T(8,128)}, f32[128,1024]{1,0:T(8,128)}, f32[128,1024]{1,0:T(8,128)}) custom-call(f32[128,1024]{1,0:T(8,128)S(1)} %get-tuple-element.11.refs_0_, f32[128,1024]{1,0:T(8,128)S(1)} %get-tuple-element.12.refs_1_, f32[128,1024]{1,0:T(8,128)S(1)} %get-tuple-element.13.refs_2_), custom_call_target="tpu_custom_call" | custom-call | tf_op jit(solution)/shard_map/hand_out/pallas_call | solution.py:394

commit v3 on v2

--- a/solution.py
+++ b/solution.py
@@ -56,13 +56,13 @@
 
 def kernel(
     q_hbm, k_hbm, v_hbm, t_hbm, gain_hbm, mask_hbm,
-    gq_out, gk_out, gv_out, loss_hbm,
-    k_all, v_all, q, k, v, t, gain, mask_row, mask, loss,
+    gq_out, gk_out, gv_out, loss_out,
+    k_all, v_all, q, k, v, t, gain, mask_row, mask,
     qh, ql, kh, kl, vh, vl, sh, sl, att, g, gq, gk, gv, acc,
     kv, kv_far, other, comb, recv, pre, part,
     qg, qg_one, comb_b, recv_b, pre_b, part_b,
     row_out, row_in, stat_z_out, stat_z, stat_y_out, stat_y,
-    load_sems, send_sems, recv_sems,
+    load_sems, store_sem, send_sems, recv_sems,
 ):
     s, x = lax.axis_index("seq"), lax.axis_index("head")
     y, z, c = s // 16, (s // 2) % ZS, s % 2
@@ -219,10 +219,14 @@
         scan(recv, pre, part, FORWARD, chunk, False)
     acc[...] = jnp.zeros_like(acc)
 
+    def stacked(high, low, i):
+        return [part_of[:, i].reshape(2 * HEAD_DIM, HEAD_DIM) for part_of in (high, low)]
+
     def attend(i, carry):
         prior = split(part[rows_of(i), :])
+        both = dot3(stacked(qh, ql, i), prior, NN)
         for b in range(2):
-            row = att[b, i] + dot3((qh[b, i], ql[b, i]), prior, NN)
+            row = att[b, i] + both[b * HEAD_DIM : (b + 1) * HEAD_DIM]
             att[b, i] = row
             acc[b] = acc[b] + row * row
             acc[2 + b] = acc[2 + b] + t[b, :, head(i)] * row
@@ -293,32 +297,36 @@
     arrived(stat_y.at[pl.ds(0, YS - 1)], STAT_Y)
     totals = jnp.sum(stat_y[...], axis=0)
     token_total = jnp.sum(totals[1:2], axis=1, keepdims=True)
-    loss[...] = jnp.sum(totals[0:1], axis=1, keepdims=True) / token_total
-    out_loss = pltpu.make_async_copy(loss, loss_hbm, load_sems.at[6])
-    out_loss.start()
+    loss_out[...] = jnp.broadcast_to(jnp.sum(totals[0:1], axis=1, keepdims=True) / token_total, loss_out.shape)
     scale = TOKENS / token_total
 
-    def store(block, out, i, sem, finished):
+    def store(block, out, i, sem):
         columns = head(c * OWN + i)
-        block[far, i] = finished(far)
         send(block.at[far, i], out.at[:, columns], sem, partner)
-        out[:, columns] = finished(c)
+        pltpu.make_async_copy(block.at[c, i], out.at[:, columns], store_sem).start()
 
     def scaled(i, carry):
-        store(gq, gq_out, i, RESULTS, lambda b: gq[b, i] * scale)
+        for b in range(2):
+            gq[b, i] = gq[b, i] * scale
+        store(gq, gq_out, i, RESULTS)
         return carry
 
     lax.fori_loop(0, OWN, scaled, 0)
 
-    def last(i, carry):
-        later = split(part_b[rows_of(i), :])
-        store(gk, gk_out, i, RESULTS + 1, lambda b: (gk[b, i] + dot3((vh[b, i], vl[b, i]), later, NT)) * scale)
-        store(gv, gv_out, i, RESULTS + 2, lambda b: (gv[b, i] + dot3((kh[b, i], kl[b, i]), later, NN)) * scale)
-        return carry
+    def last(chunk):
+        for i in range(chunk * BOTH, (chunk + 1) * BOTH):
+            later = split(part_b[rows_of(i), :])
+            grad_keys = [gk[b, i] + dot3((vh[b, i], vl[b, i]), later, NT) for b in range(2)]
+            grad_values = [gv[b, i] + dot3((kh[b, i], kl[b, i]), later, NN) for b in range(2)]
+            for b in range(2):
+                gk[b, i] = grad_keys[b] * scale
+                gv[b, i] = grad_values[b] * scale
+            store(gk, gk_out, i, RESULTS + 1)
+            store(gv, gv_out, i, RESULTS + 2)
 
     for chunk in range(CHUNKS):
         scanned(part_b, REVERSE, chunk)
-        lax.fori_loop(chunk * BOTH, (chunk + 1) * BOTH, last, 0, unroll=True)
+        last(chunk)
     for base, flat in ((FORWARD, comb), (REVERSE, comb_b)):
         for chunk in range(CHUNKS):
             sent(flat.at[all_but_one], base + OUT + chunk)
@@ -333,13 +341,15 @@
     sent(stat_y.at[pl.ds(0, YS - 1)], STAT_Y)
     for n, done in enumerate((gq, gk, gv)):
         sent(done.at[0], RESULTS + n)
+        pltpu.make_async_copy(done.at[0], done.at[0], store_sem).wait()
         arrived(done.at[0], RESULTS + n)
-    out_loss.wait()
 
 
 def hand_out(*refs):
-    given, outs, sems = refs[:3], refs[3:6], refs[6]
-    copies = [pltpu.make_async_copy(given[n], outs[n], sems.at[n]) for n in range(3)]
+    given, outs, sems, loss = refs[:4], refs[4:8], refs[8], refs[9]
+    loss[...] = given[3][0:1, 0:1]
+    copies = [pltpu.make_async_copy(loss, outs[3], sems.at[3])]
+    copies += [pltpu.make_async_copy(given[n], outs[n], sems.at[n]) for n in range(3)]
     for copy in copies:
         copy.start()
     for copy in copies:
@@ -366,11 +376,10 @@
     arrays += (norm_gain.reshape(HEADS, HEAD_DIM), valid_mask.reshape(1, HEAD_DIM))
     grad_q, grad_k, grad_v, loss = pl.pallas_call(
         kernel,
-        out_shape=(whole, whole, whole, jax.ShapeDtypeStruct((1, 1), F32)),
+        out_shape=(whole, whole, whole, jax.ShapeDtypeStruct((8, HEAD_DIM), F32)),
         in_specs=[anywhere] * 6,
-        out_specs=(vmem, vmem, vmem, anywhere),
+        out_specs=(vmem,) * 4,
         scratch_shapes=[full, full, halves, half, half, halves, tile, pltpu.VMEM((1, HEAD_DIM), jnp.int32), tiles(2)]
-        + [pltpu.VMEM((1, 1), F32)]
         + [heads16] * 8
         + [heads] * 5
         + [pltpu.VMEM((4, HEAD_DIM, HEAD_DIM), F32)]
@@ -380,7 +389,8 @@
         + [flat] * 4
         + [tile, tiles(2 * XS), tile, tiles(ZS), tile, tiles(YS)]
         + [
-            pltpu.SemaphoreType.DMA((7,)),
+            pltpu.SemaphoreType.DMA((6,)),
+            pltpu.SemaphoreType.DMA,
             pltpu.SemaphoreType.DMA((COUNT,)),
             pltpu.SemaphoreType.DMA((COUNT,)),
         ],
@@ -391,15 +401,15 @@
     )(
         *[pltpu.with_memory_space_constraint(array, pltpu.HBM) for array in arrays],
     )
-    grad_q, grad_k, grad_v = pl.pallas_call(
+    grad_q, grad_k, grad_v, loss = pl.pallas_call(
         hand_out,
-        out_shape=(whole,) * 3,
-        in_specs=[vmem] * 3,
-        out_specs=(anywhere,) * 3,
-        scratch_shapes=[pltpu.SemaphoreType.DMA((3,))],
+        out_shape=(whole, whole, whole, jax.ShapeDtypeStruct((1, 1), F32)),
+        in_specs=[vmem] * 4,
+        out_specs=(anywhere,) * 4,
+        scratch_shapes=[pltpu.SemaphoreType.DMA((4,)), pltpu.VMEM((1, 1), F32)],
         compiler_params=pltpu.CompilerParams(vmem_limit_bytes=4 * 2**20),
         name="hand_out",
-    )(grad_q, grad_k, grad_v)
+    )(grad_q, grad_k, grad_v, loss)
     return grad_q, grad_k, grad_v, loss.reshape(())
 
 

time: 55.3 us -> 53.3 us (0.964)
  between operations: 2.41 us -> 0.64 us
where the time goes in v3:
time: 53.3 us; the launch traced here: 53.2 us
  Pallas kernels  52.6 us (99%)
  between operations  0.64 us (1%)
    pallas_call x1, Pallas kernels, shards(): pl.pallas_call(kernel, out_shape=(whole, whole, whole, jax.ShapeDtypeStru...  51.4 us
    pallas_call x1, Pallas kernels, shards(): pl.pallas_call(hand_out, out_shape=(whole, whole, whole, jax.ShapeDtypeSt...  1.18 us

profile of v3, /device:TPU:1, one launch (start us, length us, event | category | flops | bytes accessed | tf_op | source)
XLA Modules:
  0.0 53.2 jit_solution(10847118816302954717)
XLA Ops:
  0.6 51.4 %linear_attention.1 = (f32[128,1024]{1,0:T(8,128)S(1)}, f32[128,1024]{1,0:T(8,128)S(1)}, f32[128,1024]{1,0:T(8,128)S(1)}, f32[8,128]{1,0:T(8,128)S(1)}) custom-call(f32[128,1024]{1,0:T(8,128)} %q_hbm.1, f32[128,1024]{1,0:T(8,128)} %k_hbm.1, f32[128,1024]{1,0:T(8,128)} %v_hbm.1, f32[128,1024]{1,0:T(8,128)} %t_hbm.1, f32[8,128]{1,0:T(8,128)} %bitcast.3, ...), custom_call_target="tpu_custom_call" | custom-call | tf_op jit(solution)/shard_map/linear_attention/pallas_call | solution.py:377
  52.0 1.2 %hand_out.1 = (f32[128,1024]{1,0:T(8,128)}, f32[128,1024]{1,0:T(8,128)}, f32[128,1024]{1,0:T(8,128)}, f32[1,1]{1,0:T(1,128)}) custom-call(f32[128,1024]{1,0:T(8,128)S(1)} %get-tuple-element.12.refs_0_, f32[128,1024]{1,0:T(8,128)S(1)} %get-tuple-element.13.refs_1_, f32[128,1024]{1,0:T(8,128)S(1)} %get-tuple-element.14.refs_2_, ...), custom_call_target="tpu_custom_call" | custom-call | tf_op jit(solution)/shard_map/hand_out/pallas_call | solution.py:404

commit v4 on v3

--- a/solution.py
+++ b/solution.py
@@ -22,10 +22,10 @@
 F32 = jnp.float32
 BF16 = jnp.bfloat16
 MESH = pl.DeviceIdType.MESH
-PAIR, OUT, BACK = 0, CHUNKS, 2 * CHUNKS
-FORWARD, REVERSE, INPUTS = 0, 3 * CHUNKS, 6 * CHUNKS
-SUMS, STAT_Z, STAT_Y, RESULTS, COUNT = INPUTS + 5, INPUTS + 6, INPUTS + 7, INPUTS + 8, INPUTS + 11
-
+PAIR, OUT, BACK = 2 * CHUNKS, 0, CHUNKS
+FORWARD, REVERSE, INPUTS = 2 * CHUNKS, 0, 5 * CHUNKS
+MASK, SUMS, STAT_Z, STAT_Y, RESULTS, COUNT = (INPUTS + n for n in range(1, 7))
+LEGS, PAIRED, HALVES, TILES, GRADS, KINDS = range(6)
 
 def ring(delta, count):
     return min(delta, count - delta)
@@ -33,7 +33,7 @@
 
 OFFSETS = sorted(
     ((dy, dz) for dy in range(YS) for dz in range(ZS) if dy or dz),
-    key=lambda o: -(ring(o[0], YS) + ring(o[1], ZS)),
+    key=lambda o: -(ring(o[0], YS) + 2 * ring(o[1], ZS)),
 )
 
 
@@ -57,17 +57,19 @@
 def kernel(
     q_hbm, k_hbm, v_hbm, t_hbm, gain_hbm, mask_hbm,
     gq_out, gk_out, gv_out, loss_out,
-    k_all, v_all, q, k, v, t, gain, mask_row, mask,
-    qh, ql, kh, kl, vh, vl, sh, sl, att, g, gq, gk, gv, acc,
-    kv, kv_far, other, comb, recv, pre, part,
-    qg, qg_one, comb_b, recv_b, pre_b, part_b,
-    row_out, row_in, stat_z_out, stat_z, stat_y_out, stat_y,
+    whole, near, given, weighted, gain, mask_row, mask,
+    qh, ql, kh, kl, vh, vl, sh, sl, att, g, grads, acc,
+    kv, kv_far, other, legs, recv, part, recv_b, part_b, qg_one,
+    row_out, stat_z_out, stat_y_out, tiles,
     load_sems, store_sem, send_sems, recv_sems,
 ):
     s, x = lax.axis_index("seq"), lax.axis_index("head")
     y, z, c = s // 16, (s // 2) % ZS, s % 2
     me = y * ZS + z
     far = 1 - c
+    comb, pre, comb_b, pre_b = (legs.at[n] for n in range(4))
+    gq, gk, gv = (grads.at[n] for n in range(3))
+    row_in, stat_z, stat_y = (tiles.at[pl.ds(first, n)] for first, n in ((0, 2 * XS), (2 * XS, ZS), (2 * XS + ZS, YS)))
 
     def at(ty, tz, tc, tx):
         return (ty * 16 + tz * 2 + tc, tx)
@@ -83,12 +85,12 @@
         return pl.ds(pl.multiple_of(i * HEAD_DIM, HEAD_DIM), HEAD_DIM)
 
     loads = [
-        pltpu.make_async_copy(k_hbm, k_all, load_sems.at[0]),
-        pltpu.make_async_copy(v_hbm, v_all, load_sems.at[1]),
-        pltpu.make_async_copy(q_hbm.at[:, heads_of(c)], q.at[c], load_sems.at[2]),
-        pltpu.make_async_copy(t_hbm.at[:, heads_of(c)], t.at[c], load_sems.at[3]),
-        pltpu.make_async_copy(gain_hbm, gain, load_sems.at[4]),
-        pltpu.make_async_copy(mask_hbm, mask_row, load_sems.at[5]),
+        pltpu.make_async_copy(k_hbm, whole.at[0], load_sems.at[0]),
+        pltpu.make_async_copy(v_hbm, whole.at[1], load_sems.at[0]),
+        pltpu.make_async_copy(q_hbm.at[:, heads_of(c)], near.at[0], load_sems.at[1]),
+        pltpu.make_async_copy(t_hbm.at[:, heads_of(c)], near.at[1], load_sems.at[1]),
+        pltpu.make_async_copy(gain_hbm, gain, load_sems.at[2]),
+        pltpu.make_async_copy(mask_hbm, mask_row, load_sems.at[3]),
     ]
     for copy in loads:
         copy.start()
@@ -97,17 +99,20 @@
     for device in greeted:
         pl.semaphore_signal(barrier, inc=1, device_id=device, device_id_type=MESH)
 
-    def send(src, dst, sem, device):
+    def loaded(ref, sem):
+        pltpu.make_async_copy(ref, ref, load_sems.at[sem]).wait()
+
+    def send(src, dst, sem, device, kind):
         pltpu.make_async_remote_copy(
-            src_ref=src, dst_ref=dst, send_sem=send_sems.at[sem], recv_sem=recv_sems.at[sem],
+            src_ref=src, dst_ref=dst, send_sem=send_sems.at[kind], recv_sem=recv_sems.at[sem],
             device_id=device, device_id_type=MESH,
         ).start()
 
     def arrived(ref, sem):
         pltpu.make_async_copy(ref, ref, recv_sems.at[sem]).wait()
 
-    def sent(ref, sem):
-        pltpu.make_async_copy(ref, ref, send_sems.at[sem]).wait()
+    def sent(ref, kind):
+        pltpu.make_async_copy(ref, ref, send_sems.at[kind]).wait()
 
     def piece(chunk, i):
         return pl.ds(pl.multiple_of(chunk * CHUNK_ROWS + i * ROWS, ROWS), ROWS)
@@ -119,7 +124,7 @@
 
     def spread(comb, recv, base, chunk):
         for ty, tz in chips:
-            send(comb.at[piece(chunk, ty * ZS + tz)], recv.at[piece(chunk, me)], base + OUT + chunk, at(ty, tz, c, x))
+            send(comb.at[piece(chunk, ty * ZS + tz)], recv.at[piece(chunk, me)], base + OUT + chunk, at(ty, tz, c, x), LEGS)
         recv[piece(chunk, me), :] = comb[piece(chunk, me), :]
 
     def scan(recv, pre, part, base, chunk, reverse):
@@ -129,23 +134,22 @@
             pre[piece(chunk, i), :] = total
             total = total + recv[piece(chunk, i), :]
         for ty, tz in chips:
-            send(pre.at[piece(chunk, ty * ZS + tz)], part.at[piece(chunk, me)], base + BACK + chunk, at(ty, tz, c, x))
+            send(pre.at[piece(chunk, ty * ZS + tz)], part.at[piece(chunk, me)], base + BACK + chunk, at(ty, tz, c, x), LEGS)
         part[piece(chunk, me), :] = pre[piece(chunk, me), :]
 
     def scanned(part, base, chunk):
         arrived(part.at[all_but_one], base + BACK + chunk)
 
-    loads[0].wait()
-    loads[1].wait()
+    loaded(whole, 0)
 
     def outer_far(i, carry):
         columns = head(far * OWN + i)
-        kv_far[i] = dot3(split(k_all[:, columns]), split(v_all[:, columns]), TN)
+        kv_far[i] = dot3(split(whole[0, :, columns]), split(whole[1, :, columns]), TN)
         return carry
 
     def outer_own(i, carry):
         columns = head(c * OWN + i)
-        key, value = split(k_all[:, columns]), split(v_all[:, columns])
+        key, value = split(whole[0, :, columns]), split(whole[1, :, columns])
         kh[c, i], kl[c, i] = key
         vh[c, i], vl[c, i] = value
         kv[i] = dot3(key, value, TN)
@@ -156,21 +160,19 @@
     pl.semaphore_wait(barrier, len(greeted))
     for chunk in range(CHUNKS):
         half = pl.ds(chunk * BOTH, BOTH)
-        send(kv_far.at[half], other.at[half], FORWARD + PAIR + chunk, partner)
+        send(kv_far.at[half], other.at[half], FORWARD + PAIR + chunk, partner, PAIRED)
     for chunk in range(CHUNKS):
         arrived(other.at[pl.ds(0, BOTH)], FORWARD + PAIR + chunk)
         for i in range(chunk * BOTH, (chunk + 1) * BOTH):
             comb[rows_of(i), :] = kv[i] + other[i]
         spread(comb, recv, FORWARD, chunk)
 
-    send(q_hbm.at[:, heads_of(far)], q.at[c], INPUTS, partner)
-    send(k_hbm.at[:, heads_of(far)], k, INPUTS + 1, partner)
-    send(v_hbm.at[:, heads_of(far)], v, INPUTS + 2, partner)
-    send(t_hbm.at[:, heads_of(far)], t.at[c], INPUTS + 3, partner)
-    loads[4].wait()
-    loads[5].wait()
+    for n, hbm in enumerate((q_hbm, k_hbm, v_hbm, t_hbm)):
+        send(hbm.at[:, heads_of(far)], given.at[n], INPUTS, partner, HALVES)
+    loaded(gain, 2)
+    loaded(mask_row, 3)
     mask[c] = jnp.broadcast_to(mask_row[...].astype(F32), (8, HEAD_DIM))
-    send(mask.at[c], mask.at[c], INPUTS + 4, partner)
+    send(mask.at[c], mask.at[c], MASK, partner, TILES)
 
     token = lax.broadcasted_iota(jnp.int32, (HEAD_DIM, HEAD_DIM), 0)
     column = lax.broadcasted_iota(jnp.int32, (HEAD_DIM, HEAD_DIM), 1)
@@ -179,38 +181,34 @@
     def as_columns(row):
         return jnp.transpose(jnp.broadcast_to(row, (HEAD_DIM, HEAD_DIM)))
 
-    def local(b, i, mask_columns):
-        query = split(q[b, :, head(i)])
+    def local(b, i, query, target, mask_columns):
+        query = split(query)
         qh[b, i], ql[b, i] = query
         scores = jnp.where(causal, dot3(query, (kh[b, i], kl[b, i]), NT), 0.0)
         scores = split(scores)
         sh[b, i], sl[b, i] = scores
         att[b, i] = dot3(scores, (vh[b, i], vl[b, i]), NN)
-        t[b, :, head(i)] = gain[pl.ds(c * OWN + i, 1), :] * (mask_columns * t[b, :, head(i)])
-
-    loads[2].wait()
-    loads[3].wait()
+        weighted[b, i] = gain[pl.ds(c * OWN + i, 1), :] * (mask_columns * target)
+
+    loaded(near, 1)
     mask_near = as_columns(mask[c, 0:1])
 
     def local_near(i, carry):
-        local(c, i, mask_near)
+        local(c, i, near[0, :, head(i)], near[1, :, head(i)], mask_near)
         return carry
 
     lax.fori_loop(0, OWN, local_near, 0)
-    arrived(q.at[0], INPUTS)
-    arrived(k, INPUTS + 1)
-    arrived(v, INPUTS + 2)
-    arrived(t.at[0], INPUTS + 3)
-    arrived(mask.at[0], INPUTS + 4)
+    arrived(given, INPUTS)
+    arrived(mask.at[0], MASK)
     mask_far = as_columns(mask[far, 0:1])
 
     def kv_zero(i):
         return jnp.where(c == 0, kv[i], other[i])
 
     def local_far(i, carry):
-        kh[far, i], kl[far, i] = split(k[:, head(i)])
-        vh[far, i], vl[far, i] = split(v[:, head(i)])
-        local(far, i, mask_far)
+        kh[far, i], kl[far, i] = split(given[1, :, head(i)])
+        vh[far, i], vl[far, i] = split(given[2, :, head(i)])
+        local(far, i, given[0, :, head(i)], given[3, :, head(i)], mask_far)
         att[1, i] = att[1, i] + dot3((qh[1, i], ql[1, i]), split(kv_zero(i)), NN)
         return carry
 
@@ -229,7 +227,7 @@
             row = att[b, i] + both[b * HEAD_DIM : (b + 1) * HEAD_DIM]
             att[b, i] = row
             acc[b] = acc[b] + row * row
-            acc[2 + b] = acc[2 + b] + t[b, :, head(i)] * row
+            acc[2 + b] = acc[2 + b] + weighted[b, i] * row
         return carry
 
     for chunk in range(CHUNKS):
@@ -239,7 +237,7 @@
     for n in range(4):
         row_out[pl.ds(n, 1), :] = jnp.sum(jnp.transpose(acc[n]), axis=0, keepdims=True)
     for device in across:
-        send(row_out, row_in.at[x * 2 + c], SUMS, device)
+        send(row_out, row_in.at[x * 2 + c], SUMS, device, TILES)
     row_in[x * 2 + c] = row_out[...]
     arrived(row_in.at[pl.ds(0, 2 * XS - 1)], SUMS)
     rows = jnp.sum(row_in[...], axis=0)
@@ -250,7 +248,7 @@
     stat_z_out[pl.ds(0, 1), :] = jnp.sum(inverse * gain_dots, axis=0, keepdims=True)
     stat_z_out[pl.ds(1, 1), :] = mask[0, 0:1] + mask[1, 0:1]
     for d in range(1, ZS):
-        send(stat_z_out, stat_z.at[z], STAT_Z, at(y, (z + d) % ZS, c, x))
+        send(stat_z_out, stat_z.at[z], STAT_Z, at(y, (z + d) % ZS, c, x), TILES)
     stat_z[z] = stat_z_out[...]
     inverse_columns = [as_columns(inverse[b : b + 1]) for b in range(2)]
     slope_columns = [as_columns(slope[b : b + 1]) for b in range(2)]
@@ -258,7 +256,7 @@
     def outer_qg(i, carry):
         outer = []
         for b in range(2):
-            grad = inverse_columns[b] * (t[b, :, head(i)] - att[b, i] * slope_columns[b])
+            grad = inverse_columns[b] * (weighted[b, i] - att[b, i] * slope_columns[b])
             g[b, i] = grad
             outer.append(dot3((qh[b, i], ql[b, i]), split(grad), TN))
         qg_one[i] = outer[1]
@@ -290,7 +288,7 @@
     arrived(stat_z.at[pl.ds(0, ZS - 1)], STAT_Z)
     stat_y_out[...] = jnp.sum(stat_z[...], axis=0)
     for d in range(1, YS):
-        send(stat_y_out, stat_y.at[y], STAT_Y, at((y + d) % YS, z, c, x))
+        send(stat_y_out, stat_y.at[y], STAT_Y, at((y + d) % YS, z, c, x), TILES)
     stat_y[y] = stat_y_out[...]
     for chunk in range(CHUNKS):
         scan(recv_b, pre_b, part_b, REVERSE, chunk, True)
@@ -300,15 +298,15 @@
     loss_out[...] = jnp.broadcast_to(jnp.sum(totals[0:1], axis=1, keepdims=True) / token_total, loss_out.shape)
     scale = TOKENS / token_total
 
-    def store(block, out, i, sem):
+    def store(block, out, i):
         columns = head(c * OWN + i)
-        send(block.at[far, i], out.at[:, columns], sem, partner)
+        send(block.at[far, i], out.at[:, columns], RESULTS, partner, GRADS)
         pltpu.make_async_copy(block.at[c, i], out.at[:, columns], store_sem).start()
 
     def scaled(i, carry):
         for b in range(2):
             gq[b, i] = gq[b, i] * scale
-        store(gq, gq_out, i, RESULTS)
+        store(gq, gq_out, i)
         return carry
 
     lax.fori_loop(0, OWN, scaled, 0)
@@ -321,28 +319,20 @@
             for b in range(2):
                 gk[b, i] = grad_keys[b] * scale
                 gv[b, i] = grad_values[b] * scale
-            store(gk, gk_out, i, RESULTS + 1)
-            store(gv, gv_out, i, RESULTS + 2)
+            store(gk, gk_out, i)
+            store(gv, gv_out, i)
 
     for chunk in range(CHUNKS):
         scanned(part_b, REVERSE, chunk)
         last(chunk)
-    for base, flat in ((FORWARD, comb), (REVERSE, comb_b)):
-        for chunk in range(CHUNKS):
-            sent(flat.at[all_but_one], base + OUT + chunk)
-            sent(flat.at[all_but_one], base + BACK + chunk)
-            if base == FORWARD:
-                sent(kv_far.at[pl.ds(0, BOTH)], base + PAIR + chunk)
-    for n in range(4):
-        sent(k, INPUTS + n)
-    sent(mask.at[0], INPUTS + 4)
-    sent(row_in.at[pl.ds(0, 2 * XS - 1)], SUMS)
-    sent(stat_z.at[pl.ds(0, ZS - 1)], STAT_Z)
-    sent(stat_y.at[pl.ds(0, YS - 1)], STAT_Y)
-    for n, done in enumerate((gq, gk, gv)):
-        sent(done.at[0], RESULTS + n)
-        pltpu.make_async_copy(done.at[0], done.at[0], store_sem).wait()
-        arrived(done.at[0], RESULTS + n)
+    sent(legs.at[:, pl.ds(0, (CHIPS - 1) * ROWS * CHUNKS)], LEGS)
+    sent(kv_far, PAIRED)
+    sent(given, HALVES)
+    sent(tiles.at[pl.ds(0, 1 + 2 * XS - 1 + ZS - 1 + YS - 1)], TILES)
+    half = grads.at[:, 0]
+    sent(half, GRADS)
+    pltpu.make_async_copy(half, half, store_sem).wait()
+    arrived(half, RESULTS)
 
 
 def hand_out(*refs):
@@ -358,9 +348,6 @@
 
 def shards(queries, key_rows, value_rows, target, norm_gain, valid_mask):
     whole = jax.ShapeDtypeStruct(queries.shape, F32)
-    full = pltpu.VMEM((HEAD_DIM, HEADS * HEAD_DIM), F32)
-    half = pltpu.VMEM((HEAD_DIM, OWN * HEAD_DIM), F32)
-    halves = pltpu.VMEM((2, HEAD_DIM, OWN * HEAD_DIM), F32)
     heads = pltpu.VMEM((2, OWN, HEAD_DIM, HEAD_DIM), F32)
     heads16 = pltpu.VMEM((2, OWN, HEAD_DIM, HEAD_DIM), BF16)
     states = pltpu.VMEM((OWN, HEAD_DIM, HEAD_DIM), F32)
@@ -368,6 +355,9 @@
 
     def tiles(count):
         return pltpu.VMEM((count, 8, HEAD_DIM), F32)
+
+    def halves(count):
+        return pltpu.VMEM((count, HEAD_DIM, OWN * HEAD_DIM), F32)
 
     tile = pltpu.VMEM((8, HEAD_DIM), F32)
     anywhere = pl.BlockSpec(memory_space=pltpu.HBM)
@@ -379,19 +369,24 @@
         out_shape=(whole, whole, whole, jax.ShapeDtypeStruct((8, HEAD_DIM), F32)),
         in_specs=[anywhere] * 6,
         out_specs=(vmem,) * 4,
-        scratch_shapes=[full, full, halves, half, half, halves, tile, pltpu.VMEM((1, HEAD_DIM), jnp.int32), tiles(2)]
+        scratch_shapes=[
+            pltpu.VMEM((2, HEAD_DIM, HEADS * HEAD_DIM), F32),
+            halves(2), halves(4), heads,
+            tile, pltpu.VMEM((1, HEAD_DIM), jnp.int32), tiles(2),
+        ]
         + [heads16] * 8
-        + [heads] * 5
-        + [pltpu.VMEM((4, HEAD_DIM, HEAD_DIM), F32)]
+        + [heads] * 2
+        + [pltpu.VMEM((3, 2, OWN, HEAD_DIM, HEAD_DIM), F32), pltpu.VMEM((4, HEAD_DIM, HEAD_DIM), F32)]
         + [states] * 3
+        + [pltpu.VMEM((4, OWN * HEAD_DIM, HEAD_DIM), F32)]
         + [flat] * 4
-        + [states] * 2
-        + [flat] * 4
-        + [tile, tiles(2 * XS), tile, tiles(ZS), tile, tiles(YS)]
+        + [states]
+        + [tile] * 3
+        + [tiles(2 * XS + ZS + YS)]
         + [
-            pltpu.SemaphoreType.DMA((6,)),
+            pltpu.SemaphoreType.DMA((4,)),
             pltpu.SemaphoreType.DMA,
-            pltpu.SemaphoreType.DMA((COUNT,)),
+            pltpu.SemaphoreType.DMA((KINDS,)),
             pltpu.SemaphoreType.DMA((COUNT,)),
         ],
         compiler_params=pltpu.CompilerParams(

time: 53.3 us -> 53.2 us (level)
  no operation moved by 1% of the time
where the time goes in v4:
time: 53.2 us; the launch traced here: 53.1 us
  Pallas kernels  52.5 us (99%)
  between operations  0.64 us (1%)
    pallas_call x1, Pallas kernels, shards(): pl.pallas_call(kernel, out_shape=(whole, whole, whole, jax.ShapeDtypeStru...  51.3 us
    pallas_call x1, Pallas kernels, shards(): pl.pallas_call(hand_out, out_shape=(whole, whole, whole, jax.ShapeDtypeSt...  1.18 us

profile of v4, /device:TPU:1, one launch (start us, length us, event | category | flops | bytes accessed | tf_op | source)
XLA Modules:
  0.0 53.1 jit_solution(8922225830368791884)
XLA Ops:
  0.6 51.3 %linear_attention.1 = (f32[128,1024]{1,0:T(8,128)S(1)}, f32[128,1024]{1,0:T(8,128)S(1)}, f32[128,1024]{1,0:T(8,128)S(1)}, f32[8,128]{1,0:T(8,128)S(1)}) custom-call(f32[128,1024]{1,0:T(8,128)} %q_hbm.1, f32[128,1024]{1,0:T(8,128)} %k_hbm.1, f32[128,1024]{1,0:T(8,128)} %v_hbm.1, f32[128,1024]{1,0:T(8,128)} %t_hbm.1, f32[8,128]{1,0:T(8,128)} %bitcast.3, ...), custom_call_target="tpu_custom_call" | custom-call | tf_op jit(solution)/shard_map/linear_attention/pallas_call | solution.py:367
  51.9 1.2 %hand_out.1 = (f32[128,1024]{1,0:T(8,128)}, f32[128,1024]{1,0:T(8,128)}, f32[128,1024]{1,0:T(8,128)}, f32[1,1]{1,0:T(1,128)}) custom-call(f32[128,1024]{1,0:T(8,128)S(1)} %get-tuple-element.12.refs_0_, f32[128,1024]{1,0:T(8,128)S(1)} %get-tuple-element.13.refs_1_, f32[128,1024]{1,0:T(8,128)S(1)} %get-tuple-element.14.refs_2_, ...), custom_call_target="tpu_custom_call" | custom-call | tf_op jit(solution)/shard_map/hand_out/pallas_call | solution.py:399

commit v5 on v4

--- a/solution.py
+++ b/solution.py
@@ -60,7 +60,7 @@
     whole, near, given, weighted, gain, mask_row, mask,
     qh, ql, kh, kl, vh, vl, sh, sl, att, g, grads, acc,
     kv, kv_far, other, legs, recv, part, recv_b, part_b, qg_one,
-    row_out, stat_z_out, stat_y_out, tiles,
+    leaving, row_out, stat_z_out, stat_y_out, tiles,
     load_sems, store_sem, send_sems, recv_sems,
 ):
     s, x = lax.axis_index("seq"), lax.axis_index("head")
@@ -155,8 +155,8 @@
         kv[i] = dot3(key, value, TN)
         return carry
 
-    lax.fori_loop(0, OWN, outer_far, 0, unroll=2)
-    lax.fori_loop(0, OWN, outer_own, 0, unroll=2)
+    lax.fori_loop(0, OWN, outer_far, 0, unroll=True)
+    lax.fori_loop(0, OWN, outer_own, 0, unroll=True)
     pl.semaphore_wait(barrier, len(greeted))
     for chunk in range(CHUNKS):
         half = pl.ds(chunk * BOTH, BOTH)
@@ -197,7 +197,7 @@
         local(c, i, near[0, :, head(i)], near[1, :, head(i)], mask_near)
         return carry
 
-    lax.fori_loop(0, OWN, local_near, 0)
+    lax.fori_loop(0, OWN, local_near, 0, unroll=2)
     arrived(given, INPUTS)
     arrived(mask.at[0], MASK)
     mask_far = as_columns(mask[far, 0:1])
@@ -212,7 +212,7 @@
         att[1, i] = att[1, i] + dot3((qh[1, i], ql[1, i]), split(kv_zero(i)), NN)
         return carry
 
-    lax.fori_loop(0, OWN, local_far, 0)
+    lax.fori_loop(0, OWN, local_far, 0, unroll=2)
     for chunk in range(CHUNKS):
         scan(recv, pre, part, FORWARD, chunk, False)
     acc[...] = jnp.zeros_like(acc)
@@ -284,7 +284,7 @@
             gv[b, i] = grad_value
         return carry
 
-    lax.fori_loop(0, OWN, local_grads, 0)
+    lax.fori_loop(0, OWN, local_grads, 0, unroll=2)
     arrived(stat_z.at[pl.ds(0, ZS - 1)], STAT_Z)
     stat_y_out[...] = jnp.sum(stat_z[...], axis=0)
     for d in range(1, YS):
@@ -298,29 +298,39 @@
     loss_out[...] = jnp.broadcast_to(jnp.sum(totals[0:1], axis=1, keepdims=True) / token_total, loss_out.shape)
     scale = TOKENS / token_total
 
-    def store(block, out, i):
-        columns = head(c * OWN + i)
-        send(block.at[far, i], out.at[:, columns], RESULTS, partner, GRADS)
-        pltpu.make_async_copy(block.at[c, i], out.at[:, columns], store_sem).start()
+    def columns_of(i):
+        return head(c * OWN + i)
+
+    def hand_over(block, out, i):
+        send(block, out.at[:, columns_of(i)], RESULTS, partner, GRADS)
 
     def scaled(i, carry):
         for b in range(2):
             gq[b, i] = gq[b, i] * scale
-        store(gq, gq_out, i)
+        hand_over(gq.at[far, i], gq_out, i)
+        pltpu.make_async_copy(gq.at[c, i], gq_out.at[:, columns_of(i)], store_sem).start()
         return carry
 
     lax.fori_loop(0, OWN, scaled, 0)
 
     def last(chunk):
-        for i in range(chunk * BOTH, (chunk + 1) * BOTH):
-            later = split(part_b[rows_of(i), :])
-            grad_keys = [gk[b, i] + dot3((vh[b, i], vl[b, i]), later, NT) for b in range(2)]
-            grad_values = [gv[b, i] + dot3((kh[b, i], kl[b, i]), later, NN) for b in range(2)]
-            for b in range(2):
-                gk[b, i] = grad_keys[b] * scale
-                gv[b, i] = grad_values[b] * scale
-            store(gk, gk_out, i)
-            store(gv, gv_out, i)
+        heads = range(chunk * BOTH, (chunk + 1) * BOTH)
+        later = [split(part_b[rows_of(i), :]) for i in heads]
+
+        def finished(b):
+            keys = [gk[b, i] + dot3((vh[b, i], vl[b, i]), r, NT) for i, r in zip(heads, later)]
+            values = [gv[b, i] + dot3((kh[b, i], kl[b, i]), r, NN) for i, r in zip(heads, later)]
+            return keys, values
+
+        for n, done in enumerate(finished(far)):
+            for i, grad in zip(heads, done):
+                leaving[n, i] = grad * scale
+        for n, out in enumerate((gk_out, gv_out)):
+            for i in heads:
+                hand_over(leaving.at[n, i], out, i)
+        for out, done in zip((gk_out, gv_out), finished(c)):
+            for i, grad in zip(heads, done):
+                out[:, columns_of(i)] = grad * scale
 
     for chunk in range(CHUNKS):
         scanned(part_b, REVERSE, chunk)
@@ -331,7 +341,7 @@
     sent(tiles.at[pl.ds(0, 1 + 2 * XS - 1 + ZS - 1 + YS - 1)], TILES)
     half = grads.at[:, 0]
     sent(half, GRADS)
-    pltpu.make_async_copy(half, half, store_sem).wait()
+    pltpu.make_async_copy(gq.at[0], gq.at[0], store_sem).wait()
     arrived(half, RESULTS)
 
 
@@ -381,6 +391,7 @@
         + [pltpu.VMEM((4, OWN * HEAD_DIM, HEAD_DIM), F32)]
         + [flat] * 4
         + [states]
+        + [heads]
         + [tile] * 3
         + [tiles(2 * XS + ZS + YS)]
         + [

time: 53.2 us -> 52.9 us (level)
  no operation moved by 1% of the time
where the time goes in v5:
time: 52.9 us; the launch traced here: 52.8 us
  Pallas kernels  52.1 us (98%)
  between operations  0.64 us (1%)
    pallas_call x1, Pallas kernels, shards(): pl.pallas_call(kernel, out_shape=(whole, whole, whole, jax.ShapeDtypeStru...  50.9 us
    pallas_call x1, Pallas kernels, shards(): pl.pallas_call(hand_out, out_shape=(whole, whole, whole, jax.ShapeDtypeSt...  1.18 us

profile of v5, /device:TPU:1, one launch (start us, length us, event | category | flops | bytes accessed | tf_op | source)
XLA Modules:
  0.0 52.8 jit_solution(9110798754188297942)
XLA Ops:
  0.6 50.9 %linear_attention.1 = (f32[128,1024]{1,0:T(8,128)S(1)}, f32[128,1024]{1,0:T(8,128)S(1)}, f32[128,1024]{1,0:T(8,128)S(1)}, f32[8,128]{1,0:T(8,128)S(1)}) custom-call(f32[128,1024]{1,0:T(8,128)} %q_hbm.1, f32[128,1024]{1,0:T(8,128)} %k_hbm.1, f32[128,1024]{1,0:T(8,128)} %v_hbm.1, f32[128,1024]{1,0:T(8,128)} %t_hbm.1, f32[8,128]{1,0:T(8,128)} %bitcast.3, ...), custom_call_target="tpu_custom_call" | custom-call | tf_op jit(solution)/shard_map/linear_attention/pallas_call | solution.py:377
  51.6 1.2 %hand_out.1 = (f32[128,1024]{1,0:T(8,128)}, f32[128,1024]{1,0:T(8,128)}, f32[128,1024]{1,0:T(8,128)}, f32[1,1]{1,0:T(1,128)}) custom-call(f32[128,1024]{1,0:T(8,128)S(1)} %get-tuple-element.12.refs_0_, f32[128,1024]{1,0:T(8,128)S(1)} %get-tuple-element.13.refs_1_, f32[128,1024]{1,0:T(8,128)S(1)} %get-tuple-element.14.refs_2_, ...), custom_call_target="tpu_custom_call" | custom-call | tf_op jit(solution)/shard_map/hand_out/pallas_call | solution.py:410

commit v6 on v5

--- a/solution.py
+++ b/solution.py
@@ -33,7 +33,7 @@
 
 OFFSETS = sorted(
     ((dy, dz) for dy in range(YS) for dz in range(ZS) if dy or dz),
-    key=lambda o: -(ring(o[0], YS) + 2 * ring(o[1], ZS)),
+    key=lambda o: -(2 * ring(o[0], YS) + 3 * ring(o[1], ZS)),
 )
 
 
@@ -76,7 +76,7 @@
 
     partner = at(y, z, far, x)
     chips = [((y + dy) % YS, (z + dz) % ZS) for dy, dz in OFFSETS]
-    across = [at(y, z, tc, (x + d) % XS) for d in (2, 1, 3) for tc in range(2)] + [partner]
+    across = [at(y, z, tc, (x + d) % XS) for d in (2, 1, 3) for tc in (far, c)] + [partner]
     greeted = [at(ty, tz, c, x) for ty, tz in chips] + across
     def heads_of(core):
         return pl.ds(pl.multiple_of(core * OWN * HEAD_DIM, HEAD_DIM), OWN * HEAD_DIM)
@@ -347,11 +347,12 @@
 
 def hand_out(*refs):
     given, outs, sems, loss = refs[:4], refs[4:8], refs[8], refs[9]
+    copies = [pltpu.make_async_copy(given[n], outs[n], sems.at[n]) for n in range(3)]
+    copies.append(pltpu.make_async_copy(loss, outs[3], sems.at[3]))
+    for copy in copies[:3]:
+        copy.start()
     loss[...] = given[3][0:1, 0:1]
-    copies = [pltpu.make_async_copy(loss, outs[3], sems.at[3])]
-    copies += [pltpu.make_async_copy(given[n], outs[n], sems.at[n]) for n in range(3)]
-    for copy in copies:
-        copy.start()
+    copies[3].start()
     for copy in copies:
         copy.wait()
 

time: 52.9 us -> 52.3 us (0.989)
    pallas_call x1, Pallas kernels: 50.9 us -> 50.4 us  [shards(): pl.pallas_call(kernel, out_shape=(whole, whole, whole, jax.ShapeDtypeStru...]
where the time goes in v6:
time: 52.3 us; the launch traced here: 52.2 us
  Pallas kernels  51.6 us (99%)
  between operations  0.64 us (1%)
    pallas_call x1, Pallas kernels, shards(): pl.pallas_call(kernel, out_shape=(whole, whole, whole, jax.ShapeDtypeStru...  50.4 us
    pallas_call x1, Pallas kernels, shards(): pl.pallas_call(hand_out, out_shape=(whole, whole, whole, jax.ShapeDtypeSt...  1.18 us

profile of v6, /device:TPU:1, one launch (start us, length us, event | category | flops | bytes accessed | tf_op | source)
XLA Modules:
  0.0 52.2 jit_solution(4797410486699348953)
XLA Ops:
  0.6 50.4 %linear_attention.1 = (f32[128,1024]{1,0:T(8,128)S(1)}, f32[128,1024]{1,0:T(8,128)S(1)}, f32[128,1024]{1,0:T(8,128)S(1)}, f32[8,128]{1,0:T(8,128)S(1)}) custom-call(f32[128,1024]{1,0:T(8,128)} %q_hbm.1, f32[128,1024]{1,0:T(8,128)} %k_hbm.1, f32[128,1024]{1,0:T(8,128)} %v_hbm.1, f32[128,1024]{1,0:T(8,128)} %t_hbm.1, f32[8,128]{1,0:T(8,128)} %bitcast.3, ...), custom_call_target="tpu_custom_call" | custom-call | tf_op jit(solution)/shard_map/linear_attention/pallas_call | solution.py:378
  51.1 1.2 %hand_out.1 = (f32[128,1024]{1,0:T(8,128)}, f32[128,1024]{1,0:T(8,128)}, f32[128,1024]{1,0:T(8,128)}, f32[1,1]{1,0:T(1,128)}) custom-call(f32[128,1024]{1,0:T(8,128)S(1)} %get-tuple-element.12.refs_0_, f32[128,1024]{1,0:T(8,128)S(1)} %get-tuple-element.13.refs_1_, f32[128,1024]{1,0:T(8,128)S(1)} %get-tuple-element.14.refs_2_, ...), custom_call_target="tpu_custom_call" | custom-call | tf_op jit(solution)/shard_map/hand_out/pallas_call | solution.py:411

commit v7 on v6

--- a/solution.py
+++ b/solution.py
@@ -76,7 +76,7 @@
 
     partner = at(y, z, far, x)
     chips = [((y + dy) % YS, (z + dz) % ZS) for dy, dz in OFFSETS]
-    across = [at(y, z, tc, (x + d) % XS) for d in (2, 1, 3) for tc in (far, c)] + [partner]
+    across = [at(y, z, tc, (x + d) % XS) for d in (1, 3, 2) for tc in (far, c)] + [partner]
     greeted = [at(ty, tz, c, x) for ty, tz in chips] + across
     def heads_of(core):
         return pl.ds(pl.multiple_of(core * OWN * HEAD_DIM, HEAD_DIM), OWN * HEAD_DIM)

time: 52.3 us -> 52.4 us (level)
  no operation moved by 1% of the time
where the time goes in v7:
time: 52.4 us; the launch traced here: 52.3 us
  Pallas kernels  51.7 us (99%)
  between operations  0.64 us (1%)
    pallas_call x1, Pallas kernels, shards(): pl.pallas_call(kernel, out_shape=(whole, whole, whole, jax.ShapeDtypeStru...  50.5 us
    pallas_call x1, Pallas kernels, shards(): pl.pallas_call(hand_out, out_shape=(whole, whole, whole, jax.ShapeDtypeSt...  1.18 us

profile of v7, /device:TPU:1, one launch (start us, length us, event | category | flops | bytes accessed | tf_op | source)
XLA Modules:
  0.0 52.3 jit_solution(9463257302295667130)
XLA Ops:
  0.6 50.5 %linear_attention.1 = (f32[128,1024]{1,0:T(8,128)S(1)}, f32[128,1024]{1,0:T(8,128)S(1)}, f32[128,1024]{1,0:T(8,128)S(1)}, f32[8,128]{1,0:T(8,128)S(1)}) custom-call(f32[128,1024]{1,0:T(8,128)} %q_hbm.1, f32[128,1024]{1,0:T(8,128)} %k_hbm.1, f32[128,1024]{1,0:T(8,128)} %v_hbm.1, f32[128,1024]{1,0:T(8,128)} %t_hbm.1, f32[8,128]{1,0:T(8,128)} %bitcast.3, ...), custom_call_target="tpu_custom_call" | custom-call | tf_op jit(solution)/shard_map/linear_attention/pallas_call | solution.py:378
  51.2 1.2 %hand_out.1 = (f32[128,1024]{1,0:T(8,128)}, f32[128,1024]{1,0:T(8,128)}, f32[128,1024]{1,0:T(8,128)}, f32[1,1]{1,0:T(1,128)}) custom-call(f32[128,1024]{1,0:T(8,128)S(1)} %get-tuple-element.12.refs_0_, f32[128,1024]{1,0:T(8,128)S(1)} %get-tuple-element.13.refs_1_, f32[128,1024]{1,0:T(8,128)S(1)} %get-tuple-element.14.refs_2_, ...), custom_call_target="tpu_custom_call" | custom-call | tf_op jit(solution)/shard_map/hand_out/pallas_call | solution.py:411
